TPU v7x, 128 devices: a whole 4x4x4 slice. The times are simulated.
128 devices in a mesh: ctx: 32 (over x, y, core), row: 4 (over z).
Axes of the slice: x: 4, y: 4, z: 4, core: 2. Of those that a mesh axis runs over, the one named last changes fastest.
Arguments:
- latent_cache: bfloat16 [131072, 576], P(('ctx', 'row')), may hold values from -8 to 8
- index_keys: bfloat16 [131072, 128], P('ctx'), may hold values from -6 to 6
- query_latent: bfloat16 [512, 128, 576], P(('row', 'ctx')), may hold values from -100 to 99
- index_query: bfloat16 [512, 64, 128], P(('row', 'ctx')), may hold values from -0.5 to 0.5
- index_gates: bfloat16 [512, 64], P(('row', 'ctx')), may hold values from -0.75 to 0.75
- selected: int32 [512, 2048], P(('row', 'ctx')), may hold values from 0 to 131071, as said below
Outputs:
- attended: bfloat16 [512, 128, 512], P(('row', 'ctx'))
- index_scores: float32 [512, 131072], P('row', 'ctx')
Inputs may be any that keep to these rules, and one draw needn't show every extreme that they name: `selected`: each row names 2048 different tokens. Among the tokens of one index of ctx (s * 4096 <= t < (s + 1) * 4096) a row names at most 256, and exactly 256 in one such range; a row names at most one token in each aligned run of 16 tokens.
All inputs are finite; a program needn't handle non-finite values.
Results may differ from a plain program's by a relative error of at most 0.0045.
Values may be sent and summed in bfloat16 or wider, within the bound.
A program may use at most 256 MiB of HBM per device.

v0:
```python
import jax
import jax.numpy as jnp
from jax import lax
from jax.sharding import PartitionSpec as P

LATENT = 512
SCORE_DIM = 192
SEL_MOST = 256
TOK_DEV = 4096


def index_block(iquery, gates, index_keys):
    count = iquery.shape[0]
    groups = count // 8
    heads = iquery.shape[1]
    query_blocks = iquery.reshape(groups, 8 * heads, iquery.shape[2])
    gate_blocks = gates.astype(jnp.float32).reshape(groups, 8, heads)

    def one_block(pair):
        block, gate = pair
        logits = jnp.einsum("qd,td->qt", block, index_keys, preferred_element_type=jnp.float32)
        logits = logits.reshape(8, heads, logits.shape[1])
        return jnp.sum(gate[:, :, None] * jnp.maximum(logits, 0.0), axis=1)

    result = lax.map(one_block, (query_blocks, gate_blocks))
    return result.reshape(count, result.shape[2])


def slot_table(place, value, slots):

    def one_row(pair):
        where_to, what = pair
        hit = where_to[:, None] == jnp.arange(slots, dtype=jnp.int32)[None, :]
        return jnp.max(jnp.where(hit, what[:, None], -1), axis=0)

    return lax.map(one_row, (place, value))


def pick_rows(source, table, spacing):
    blocks = source.reshape(source.shape[0] // spacing, spacing, source.shape[1])
    offset = table % spacing
    onehot = (
        (offset[:, :, None] == jnp.arange(spacing, dtype=jnp.int32)[None, None, :])
        & (table >= 0)[:, :, None]
    ).astype(jnp.bfloat16)
    rows_out = jnp.einsum("gsj,sjd->gsd", onehot, blocks, preferred_element_type=jnp.float32)
    return rows_out.astype(jnp.bfloat16)


def weigh(queries, keys, valid):
    scores = jnp.einsum(
        "ghd,gsd->ghs", queries, keys, preferred_element_type=jnp.float32
    ) * SCORE_DIM ** (-0.5)
    return jnp.where(valid[:, None, :], scores, -1e30)


def combine(masked, peak, keys, valid):
    weights = jnp.where(valid[:, None, :], jnp.exp(masked - peak[:, :, None]), 0.0).astype(
        jnp.bfloat16
    )
    totals = jnp.sum(weights.astype(jnp.float32), axis=2)
    sums = jnp.einsum(
        "ghs,gsd->ghd", weights, keys[:, :, :LATENT], preferred_element_type=jnp.float32
    )
    return (sums, totals)


def body(latent_cache, index_keys, query_latent, index_query, index_gates, selected):
    spacing = TOK_DEV // SEL_MOST
    slab = lax.all_gather(latent_cache, "row", axis=0, tiled=True)
    queries, iquery, gates = (
        lax.all_gather(query_latent, "ctx", axis=0, tiled=True),
        lax.all_gather(index_query, "ctx", axis=0, tiled=True),
        lax.all_gather(index_gates, "ctx", axis=0, tiled=True),
    )
    picks = lax.all_gather(selected, "ctx", axis=0, tiled=True)
    index_scores = index_block(iquery, gates, index_keys)
    local = picks - lax.axis_index("ctx") * TOK_DEV
    mine = (local >= 0) & (local < TOK_DEV)
    place = jnp.where(mine, local // spacing, SEL_MOST)
    table = slot_table(place, local, SEL_MOST)
    valid = table >= 0
    keys = pick_rows(slab, table, spacing)
    masked = weigh(queries, keys, valid)
    peak = lax.pmax(jnp.max(masked, axis=2), "ctx")
    sums, totals = combine(masked, peak, keys, valid)
    summed, total = (
        lax.psum_scatter(sums, "ctx", scatter_dimension=0, tiled=True),
        lax.psum_scatter(totals, "ctx", scatter_dimension=0, tiled=True),
    )
    attended = (summed / total[:, :, None]).astype(jnp.bfloat16)
    return (attended, index_scores)


def solution(mesh):
    return jax.shard_map(
        body,
        mesh=mesh,
        in_specs=(
            P(("ctx", "row"), None),
            P("ctx", None),
            P(("row", "ctx"), None, None),
            P(("row", "ctx"), None, None),
            P(("row", "ctx"), None),
            P(("row", "ctx"), None),
        ),
        out_specs=(P(("row", "ctx"), None, None), P("row", "ctx")),
        check_vma=False,
    )
```

profile of v0, /device:TPU:6, one launch (start us, length us, event | category | flops | bytes accessed | tf_op | source)
XLA Modules:
  0.0 750.1 jit_solution(6434805967596199768)
XLA Ops:
  9.4 45.2 %all-gather.13.cloned.1.call-done = s32[32,4,2048]{2,1,0:T(4,128)} async-done(((s32[1,4,2048]{2,1,0:T(4,128)}), s32[32,4,2048]{2,1,0:T(4,128)}) %all-gather.13.cloned.1.call-update) | async-done | bytes 1048592 | tf_op jit(solution)/shard_map/all_gather | solution.py:76
  54.7 1.3 broadcast_subtract_fusion
  57.1 166.7 %while.22 = (s32[]{:T(128)}, s32[128,256]{1,0:T(8,128)S(1)}, s32[128,2048]{1,0:T(8,128)S(1)}, s32[128,2048]{1,0:T(8,128)S(1)}) while((s32[]{:T(128)}, s32[128,256]{1,0:T(8,128)S(1)}, s32[128,2048]{1,0:T(8,128)S(1)}, s32[128,2048]{1,0:T(8,128)S(1)}) %tuple.46), condition=%wide.region_2.3_spmd.clone, body=%wide.region_0.2_spmd.sunk.clone | while | flops 1572610 | bytes 52293 | solution.py:36
  57.1 1.2 select_reduce_fusion.3
  58.4 1.2 select_reduce_fusion.3
  59.7 1.2 select_reduce_fusion.3
  61.0 1.2 select_reduce_fusion.3
  62.3 1.2 select_reduce_fusion.3
  63.6 1.2 select_reduce_fusion.3
  64.9 1.2 select_reduce_fusion.3
  66.2 1.2 select_reduce_fusion.3
  67.5 1.2 select_reduce_fusion.3
  68.8 1.2 select_reduce_fusion.3
  70.1 1.2 select_reduce_fusion.3
  71.4 1.2 select_reduce_fusion.3
  72.8 1.2 select_reduce_fusion.3
  74.1 1.2 select_reduce_fusion.3
  75.4 1.2 select_reduce_fusion.3
  224.2 7.6 %copy.22 = bf16[4096,576]{1,0:T(8,128)(2,1)} copy(bf16[4096,576]{0,1:T(8,128)(2,1)} %all-gather.7.cloned.1.call-done) | data formatting | bytes 9437184 | tf_op jit(solution)/shard_map/all_gather | solution.py:70
  231.8 18.0 %convert_bitcast_fusion = bf16[128,256,576]{0,2,1:T(8,128)(2,1)} fusion(bf16[256,16,576]{2,1,0:T(8,128)(2,1)} %bitcast.69, s32[128,256]{0,1:T(8,128)S(1)} %copy.20, pred[128,256]{0,1:T(8,128)(4,1)S(1)} %copy.21), kind=kOutput, calls=%fused_computation.9 | convolution fusion | flops 623902720 | bytes 42631168 | tf_op jit(solution)/shard_map/gsj,sjd->gsd/dot_general | solution.py:46
  249.8 51.8 %copy.23 = bf16[128,256,576]{1,2,0:T(8,128)(2,1)} copy(bf16[128,256,576]{0,2,1:T(8,128)(2,1)} %convert_bitcast_fusion) | data formatting | bytes 75497472 | tf_op jit(solution)/shard_map/convert_element_type | solution.py:47
  301.7 30.3 %bitcast_reduce_fusion = (f32[128,128]{1,0:T(8,128)}, f32[128,256,128]{2,1,0:T(8,128)}) fusion(pred[128,256]{1,0:T(8,128)(4,1)S(1)} %broadcast_compare_fusion, bf16[128,256,576]{1,2,0:T(8,128)(2,1)} %copy.23, bf16[128,128,576]{1,2,0:T(8,128)(2,1)} %all-gather.9.cloned.1.call-done), kind=kOutput, calls=%fused_computation.11 | convolution fusion | flops 4844404736 | bytes 73498624 | tf_op jit(solution)/shard_map/ghd,gsd->ghs/dot_general | solution.py:51
  332.6 23.0 %slice.4 = bf16[128,256,512]{0,2,1:T(8,128)(2,1)} slice(bf16[128,256,576]{0,2,1:T(8,128)(2,1)} %convert_bitcast_fusion), slice={[0:128], [0:256], [0:512]} | slice | bytes 67108864 | tf_op jit(solution)/shard_map/slice | solution.py:63
  355.6 44.9 %copy.25 = bf16[128,256,512]{2,1,0:T(8,128)(2,1)} copy(bf16[128,256,512]{0,2,1:T(8,128)(2,1)} %slice.4) | data formatting | bytes 67108864 | tf_op jit(solution)/shard_map/slice | solution.py:63
  400.5 27.3 %all-reduce.4.cloned.1.call-done = f32[128,128]{1,0:T(8,128)} async-done(((f32[128,128]{1,0:T(8,128)}), f32[128,128]{1,0:T(8,128)}) %all-reduce.4.cloned.1.call-update) | async-done | bytes 65552 | tf_op jit(solution)/shard_map/pmax | solution.py:85
  427.8 14.2 %convert_reduce_fusion = f32[128,128]{1,0:T(8,128)} fusion(f32[128,128]{1,0:T(8,128)} %all-reduce.4.cloned.1.call-done, f32[128,256,128]{2,1,0:T(8,128)} %get-tuple-element.74, pred[128,256]{1,0:T(8,128)(4,1)S(1)} %broadcast_compare_fusion), kind=kLoop, calls=%fused_computation.15 | loop fusion | flops 29343744 | bytes 16941056 | tf_op jit(solution)/shard_map/reduce_sum | solution.py:61
  442.2 32.7 %fusion.12 = f32[128,128,512]{2,1,0:T(8,128)} fusion(bf16[128,256,512]{2,1,0:T(8,128)(2,1)} %copy.25, f32[128,256,128]{2,1,0:T(8,128)} %get-tuple-element.74, f32[128,128]{1,0:T(8,128)S(1)} %copy-done, pred[128,256]{1,0:T(8,128)(4,1)S(1)} %broadcast_compare_fusion), kind=kOutput, calls=%fused_computation.38 | convolution fusion | flops 4315938816 | bytes 83984384 | tf_op jit(solution)/shard_map/ghs,gsd->ghd/dot_general | solution.py:62
  476.9 22.5 %all-gather.1 = bf16[32,4,64]{2,1,0:T(4,128)(2,1)S(1)} all-gather(bf16[1,4,64]{2,1,0:T(4,128)(2,1)S(1)} %bitcast.79), channel_id=1, replica_groups=mesh['ctx'=32,'row'=4] {'ctx'}, dimensions={0}, use_global_device_ids=true | all-gather | bytes 16896 | tf_op jit(solution)/shard_map/all_gather | solution.py:74
  499.4 46.3 %while.23 = (s32[]{:T(128)}, f32[16,8,4096]{2,1,0:T(8,128)}, f32[16,8,64]{2,1,0:T(8,128)S(1)}, bf16[16,512,128]{2,1,0:T(8,128)(2,1)}, bf16[4096,128]{1,0:T(8,128)(2,1)S(1)}) while((s32[]{:T(128)}, f32[16,8,4096]{2,1,0:T(8,128)}, f32[16,8,64]{2,1,0:T(8,128)S(1)}, bf16[16,512,128]{2,1,0:T(8,128)(2,1)}, ...), condition=%wide.region_10.11_spmd.clone, body=%wide.region_8.10_spmd.sunk.clone | while | flops 543129600 | bytes 1841233 | solution.py:25
  500.4 1.3 multiply_reduce_fusion.3
  503.3 1.3 multiply_reduce_fusion.3
  506.2 1.3 multiply_reduce_fusion.3
  509.1 1.3 multiply_reduce_fusion.3
  511.9 1.3 multiply_reduce_fusion.3
  514.8 1.3 multiply_reduce_fusion.3
  517.7 1.3 multiply_reduce_fusion.3
  520.6 1.3 multiply_reduce_fusion.3
  523.5 1.3 multiply_reduce_fusion.3
  526.4 1.3 multiply_reduce_fusion.3
  529.3 1.3 multiply_reduce_fusion.3
  532.2 1.3 multiply_reduce_fusion.3
  535.1 1.3 multiply_reduce_fusion.3
  538.0 1.3 multiply_reduce_fusion.3
  540.9 1.3 multiply_reduce_fusion.3
  543.8 1.3 multiply_reduce_fusion.3
  545.8 26.5 %all-reduce.6.cloned.1.call-done = f32[128,128]{1,0:T(8,128)} async-done(((f32[128,128]{1,0:T(8,128)}), f32[128,128]{1,0:T(8,128)}) %all-reduce.6.cloned.1.call-update) | async-done | bytes 65552
  572.9 168.1 %reduce-scatter.2.cloned.1.call-done = f32[4,128,512]{2,1,0:T(8,128)} async-done(((f32[128,128,512]{2,1,0:T(8,128)}), f32[4,128,512]{2,1,0:T(8,128)}) %reduce-scatter.2.cloned.1.call-update) | async-done | bytes 1048592 | tf_op jit(solution)/shard_map/reduce_scatter | solution.py:88
  741.1 2.2 divide_convert_fusion
  (453 shorter events, 176.6 us)
Async XLA Ops:
  7.2 47.5 %all-gather.13.cloned.1.call-start = ((), (), s32[]{:S(2)}) async-start(), calls=%async_computation.6 | async-start | bytes 1081344 | tf_op jit(solution)/shard_map/all_gather | solution.py:76
  7.9 216.3 %all-gather.7.cloned.1.call-start = ((), (), s32[]{:S(2)}) async-start(), calls=%async_computation.1 | async-start | bytes 5898240 | tf_op jit(solution)/shard_map/all_gather | solution.py:70
  8.6 293.0 %all-gather.9.cloned.1.call-start = ((), (), s32[]{:S(2)}) async-start(), calls=%async_computation.2 | async-start | bytes 19464192 | tf_op jit(solution)/shard_map/all_gather | solution.py:72
  9.4 418.4 %all-reduce.4.cloned.1.call-start = ((), (), s32[]{:S(2)}) async-start(), calls=%async_computation.3 | async-start | bytes 131072 | tf_op jit(solution)/shard_map/pmax | solution.py:85
  332.0 167.4 %all-gather.11.cloned.1.call-start = ((), (), s32[]{:S(2)}) async-start(), calls=%async_computation.5 | async-start | bytes 2162688 | tf_op jit(solution)/shard_map/all_gather | solution.py:73
  332.6 239.7 %all-reduce.6.cloned.1.call-start = ((), (), s32[]{:S(2)}) async-start(), calls=%async_computation.7 | async-start | bytes 131072
  427.8 14.5 %copy-start = (f32[128,128]{1,0:T(8,128)S(1)}, f32[128,128]{1,0:T(8,128)}, u32[]{:S(2)}) copy-start(f32[128,128]{1,0:T(8,128)} %all-reduce.4.cloned.1.call-done) | copy-start | bytes 196612
  442.0 299.1 %reduce-scatter.2.cloned.1.call-start = ((), (), s32[]{:S(2)}) async-start(), calls=%async_computation.4 | async-start | bytes 34603008 | tf_op jit(solution)/shard_map/reduce_scatter | solution.py:88
  475.0 0.7 copy-start.3
  475.0 1.9 copy-start.1
  475.0 24.4 %copy-start.2 = (bf16[4096,128]{1,0:T(8,128)(2,1)S(1)}, bf16[4096,128]{1,0:T(8,128)(2,1)}, u32[]{:S(2)}) copy-start(bf16[4096,128]{1,0:T(8,128)(2,1)} %param.11) | copy-start | bytes 3145732
Sparse Core Ops, SparseCore 0:
  10.2 44.3 all-gather.12
  56.3 52.4 all-gather.6
  111.1 77.5 all-gather.8
  332.1 95.6 all-reduce.3
  429.9 42.9 all-gather.10
  476.5 95.6 all-reduce.5
  576.2 164.8 reduce-scatter.1
where the time goes:
time: 754 us; the launch traced here: 750 us
  waiting for transfers between devices  270 us (36%)
  other arithmetic  173 us (23%)
  local copies, waits for them, and re-layouts  163 us (22%)
  matrix products  102 us (14%)
  blocking collectives  22.5 us (3%)
  between operations  14.9 us (2%)
    reduce_scatter x1, waiting for transfers between devices, body(): lax.psum_scatter(sums, 'ctx', scatter_dimension=0, tiled=True)  168 us
    reduce_max x128, other arithmetic, one_row(): return jnp.max(jnp.where(hit, what[:, None], -1), axis=0)  155 us
    slice x2, local copies, waits for them, and re-layouts, combine(): keys[:, :, :LATENT]  67.9 us
    convert_element_type x1, local copies, waits for them, and re-layouts, pick_rows(): return rows_out.astype(jnp.bfloat16)  51.8 us
    all_gather x1, waiting for transfers between devices, body(): picks = lax.all_gather(selected, 'ctx', axis=0, tiled=True)  45.2 us
    dot_general x1, matrix products, combine(): jnp.einsum('ghs,gsd->ghd', weights, keys[:, :, :LATENT], preferred_elemen...  32.7 us
    dot_general x1, matrix products, weigh(): jnp.einsum('ghd,gsd->ghs', queries, keys, preferred_element_type=jnp.floa...  30.3 us
    unnamed x8, waiting for transfers between devices  29.2 us
  transfers between devices with their start and end apart: 7, of which 4 were waited for; matrix products, arithmetic and copies ran while one was open for 54% of the time, Pallas kernels for 0%

commit v1 on v0

v1 whole, which is shorter than its diff:
```python
import jax
import jax.numpy as jnp
from jax import lax
from jax.experimental import pallas as pl
from jax.experimental.pallas import tpu as pltpu
from jax.sharding import PartitionSpec as P

MESH = pl.DeviceIdType.MESH
LATENT = 512
SCALE = 192 ** (-0.5)
NONE = -1e30
FLOOR = -1e29
F32 = jnp.float32
BF16 = jnp.bfloat16
NT = (((1,), (1,)), ((), ()))


def remote(src, dst, send, recv, device):
    return pltpu.make_async_remote_copy(
        src_ref=src, dst_ref=dst, send_sem=send, recv_sem=recv, device_id=device, device_id_type=MESH
    )


def place(core):
    chip = lax.axis_index("ctx") // 2
    x, y = chip // 4, chip % 4
    return x * (1 - core) + y * core, y * (1 - core) + x * core


def chip_of(a, b, core):
    a, b = a % 4, b % 4
    return (a * (1 - core) + b * core) * 4 + b * (1 - core) + a * core


class Ring:
    def __init__(self, own, buf, rows, send, recv, core, on_block=None):
        self.own, self.buf, self.send, self.recv, self.core = own, buf, send, recv, core
        self.halves = (pl.ds(0, rows), pl.ds(0, rows // 2), pl.ds(rows // 2, rows // 2))
        self.a, self.b = place(core)
        self.columns = (self.a, self.a + 3, self.a + 1, self.a + 2)
        self.sent = []
        self.on_block = on_block

    def view(self, a, b, part):
        return self.buf(chip_of(a, b, self.core), self.halves[part])

    def put(self, k, block, part, to, own=False):
        src = self.own if own else self.view(*block, part)
        device = {"ctx": chip_of(*to, self.core) * 2 + self.core}
        copy = remote(src, self.view(*block, part), self.send.at[k], self.recv.at[k], device)
        copy.start()
        self.sent.append(copy)

    def get(self, k, block, part, event):
        ref = self.view(*block, part)
        remote(ref, ref, self.send.at[k], self.recv.at[k], {"ctx": lax.axis_index("ctx")}).wait_recv()
        if self.on_block is not None:
            self.on_block(event, block, part)

    def start(self):
        a, b = self.a, self.b
        self.put(4, (a, b), 0, (a, b + 1), own=True)
        self.put(5, (a, b), 0, (a, b + 3), own=True)
        self.put(0, (a, b), 0, (a + 1, b), own=True)
        self.put(1, (a, b), 0, (a + 3, b), own=True)

    def second(self, j):
        block = (self.columns[j], self.b)
        self.put(4 + 4 * j, block, 0, (self.a, self.b + 1))
        self.put(5 + 4 * j, block, 0, (self.a, self.b + 3))

    def near(self):
        a, b = self.a, self.b
        self.get(0, (a + 3, b), 0, 1)
        self.put(2, (a + 3, b), 1, (a + 1, b))
        self.second(1)
        self.get(1, (a + 1, b), 0, 2)
        self.put(3, (a + 1, b), 2, (a + 3, b))
        self.second(2)

    def far(self):
        a, b = self.a, self.b
        self.get(2, (a + 2, b), 1, 3)
        self.get(3, (a + 2, b), 2, 4)
        self.second(3)

    def relay(self, j):
        column, b = self.columns[j], self.b
        self.get(4 + 4 * j, (column, b + 3), 0, 5 + 4 * j)
        self.put(6 + 4 * j, (column, b + 3), 1, (self.a, b + 1))
        self.get(5 + 4 * j, (column, b + 1), 0, 6 + 4 * j)
        self.put(7 + 4 * j, (column, b + 1), 2, (self.a, b + 3))

    def last(self, j):
        column, b = self.columns[j], self.b
        self.get(6 + 4 * j, (column, b + 2), 1, 7 + 4 * j)
        self.get(7 + 4 * j, (column, b + 2), 2, 8 + 4 * j)

    def finish(self):
        for copy in self.sent:
            copy.wait_send()


def gather_kernel(
    q_ref, k_ref, iq_ref, keys_ref, sel_ref,
    qall, kall, tall, isc_ref,
    iqall, tsend, gate_ref,
    q_send, q_recv, i_send, i_recv, p_send, p_recv, k_send, k_recv, t_send, t_recv, local,
):
    ctx, z = lax.axis_index("ctx"), lax.axis_index("row")
    core, chip = ctx % 2, ctx // 2
    other = 1 - core
    partner = {"ctx": chip * 2 + other}

    barrier = pltpu.get_barrier_semaphore()
    for step in range(1, 16):
        pl.semaphore_signal(
            barrier, inc=1, device_id={"ctx": ((chip + step) % 16) * 2 + core}, device_id_type=MESH
        )
    pl.semaphore_signal(barrier, inc=1, device_id=partner, device_id_type=MESH)
    for step in (1, 3):
        pl.semaphore_signal(barrier, inc=1, device_id={"row": (z + step) % 4}, device_id_type=MESH)

    def add_picks(i, total):
        token = sel_ref[pl.ds(i, 1), :]
        to = (token >> 13) * 16 + ((token >> 4) & 15)
        window = (i // 4) * 32 + ((token >> 8) & 31)
        value = ((token & 255) + 1).astype(F32)
        width = token.shape[1]
        left = lax.broadcasted_iota(jnp.int32, (256, width), 0) == to
        right = lax.broadcasted_iota(jnp.int32, (128, width), 0) == window
        return total + lax.dot_general(
            jnp.where(left, 1.0, 0.0).astype(BF16),
            jnp.where(right, value, 0.0).astype(BF16),
            NT,
            preferred_element_type=F32,
        )

    table = lax.fori_loop(0, sel_ref.shape[0], add_picks, jnp.zeros((256, 128), F32))
    tsend[...] = table.astype(BF16).reshape(16, 16, 128)

    pl.semaphore_wait(barrier, 18)

    to_partner = []

    def hand_on(event, block, part):
        ref = index_ring.view(*block, part)
        copy = remote(ref, ref, p_send.at[event], p_recv.at[event], partner)
        copy.start()
        to_partner.append(copy)

    index_ring = Ring(
        iq_ref, lambda p, rows: iqall.at[p, core, rows], iq_ref.shape[0], i_send, i_recv, core, hand_on
    )
    index_ring.start()
    copy = remote(iq_ref, iqall.at[chip, core], p_send.at[0], p_recv.at[0], partner)
    copy.start()
    to_partner.append(copy)

    table_copies = []
    for step in range(1, 16):
        to = (chip + step) % 16
        copy = remote(
            tsend.at[to], tall.at[chip], t_send.at[step], t_recv.at[step], {"ctx": to * 2 + core}
        )
        copy.start()
        table_copies.append(copy)

    k_rows = k_ref.shape[0]
    parts = (pl.ds(0, k_rows), pl.ds(0, k_rows // 2), pl.ds(k_rows // 2, k_rows // 2))
    k_sent = []

    def k_view(depth, part, c=core):
        return kall.at[c * 4 + depth % 4, parts[part]]

    def k_put(k, src, dst, device):
        copy = remote(src, dst, k_send.at[k], k_recv.at[k], device)
        copy.start()
        k_sent.append(copy)

    def k_get(k, depth, part, c=core):
        ref = k_view(depth, part, c)
        remote(ref, ref, k_send.at[k], k_recv.at[k], {"row": z}).wait_recv()

    up, down = {"row": (z + 1) % 4}, {"row": (z + 3) % 4}
    k_put(0, k_ref, k_view(z, 0), up)
    k_put(1, k_ref, k_view(z, 0), down)
    k_put(4, k_ref, k_view(z, 0), partner)

    query_ring = Ring(q_ref, lambda p, rows: qall.at[p, rows], q_ref.shape[0], q_send, q_recv, core)
    query_ring.start()

    own = [
        pltpu.make_async_copy(q_ref, qall.at[chip], local.at[0]),
        pltpu.make_async_copy(k_ref, k_view(z, 0), local.at[1]),
        pltpu.make_async_copy(tsend.at[chip], tall.at[chip], local.at[2]),
        pltpu.make_async_copy(iq_ref, iqall.at[chip, core], local.at[3]),
    ]
    for copy in own:
        copy.start()

    index_ring.near()
    index_ring.relay(0)
    index_ring.far()
    index_ring.relay(1)
    index_ring.relay(2)
    index_ring.last(0)
    index_ring.relay(3)
    for j in (1, 2, 3):
        index_ring.last(j)

    oa, ob = place(other)
    columns = (oa, oa + 3, oa + 1, oa + 2)
    arrivals = [(0, (oa, ob), 0), (1, (oa + 3, ob), 0), (2, (oa + 1, ob), 0), (3, (oa + 2, ob), 1), (4, (oa + 2, ob), 2)]
    for j in range(4):
        column = columns[j]
        arrivals += [
            (5 + 4 * j, (column, ob + 3), 0),
            (6 + 4 * j, (column, ob + 1), 0),
            (7 + 4 * j, (column, ob + 2), 1),
            (8 + 4 * j, (column, ob + 2), 2),
        ]
    for event, block, part in arrivals:
        ref = iqall.at[chip_of(*block, other), other, index_ring.halves[part]]
        remote(ref, ref, p_send.at[event], p_recv.at[event], partner).wait_recv()
    own[3].wait()

    tile = 512

    def index_chip(p, carry):
        for c in range(2):
            gates = iqall[p, c, 256:320, :].astype(F32)
            for r in range(4):
                gate_ref[pl.ds((c * 4 + r) * 64, 64), :] = jnp.broadcast_to(gates[:, r : r + 1], (64, 128))
        queries = iqall[p, :, 0:256, :].reshape(512, 128)

        def some_tokens(t, carry):
            at = pl.ds(pl.multiple_of(t * tile, tile), tile)
            logits = lax.dot_general(queries, keys_ref[at, :], NT, preferred_element_type=F32)
            rows = []
            for i in range(8):
                gate = jnp.concatenate([gate_ref[pl.ds(i * 64, 64), :]] * (tile // 128), axis=1)
                part = jnp.maximum(logits[i * 64 : (i + 1) * 64, :], 0.0) * gate
                rows.append(jnp.sum(part, axis=0, keepdims=True))
            isc_ref[pl.ds(pl.multiple_of(p * 8, 8), 8), at] = jnp.concatenate(rows, axis=0)
            return carry

        return lax.fori_loop(0, keys_ref.shape[0] // tile, some_tokens, carry)

    def index_chips(low, high):
        lax.fori_loop(low, high, index_chip, 0)

    index_chips(0, 2)
    query_ring.near()
    query_ring.relay(0)
    index_chips(2, 6)
    k_get(0, z + 3, 0)
    k_put(2, k_view(z + 3, 1), k_view(z + 3, 1), up)
    k_put(5, k_view(z + 3, 0), k_view(z + 3, 0), partner)
    k_get(1, z + 1, 0)
    k_put(3, k_view(z + 1, 2), k_view(z + 1, 2), down)
    k_put(6, k_view(z + 1, 0), k_view(z + 1, 0), partner)
    query_ring.far()
    index_chips(6, 9)
    query_ring.relay(1)
    query_ring.relay(2)
    index_chips(9, 13)
    k_get(2, z + 2, 1)
    k_put(7, k_view(z + 2, 1), k_view(z + 2, 1), partner)
    k_get(3, z + 2, 2)
    k_put(8, k_view(z + 2, 2), k_view(z + 2, 2), partner)
    query_ring.relay(3)
    index_chips(13, 16)

    for j in range(4):
        query_ring.last(j)
    k_get(4, z, 0, other)
    k_get(5, z + 3, 0, other)
    k_get(6, z + 1, 0, other)
    k_get(7, z + 2, 1, other)
    k_get(8, z + 2, 2, other)
    for step in range(1, 16):
        frm = (chip + 16 - step) % 16
        remote(
            tall.at[frm], tall.at[frm], t_send.at[step], t_recv.at[step], partner
        ).wait_recv()
    for copy in own[:3]:
        copy.wait()
    query_ring.finish()
    index_ring.finish()
    for copy in to_partner + table_copies + k_sent:
        copy.wait_send()


def attend_kernel(
    qall, kall, tall, out_ref,
    kext, ksel, qbuf, picks, mlcol, mlin,
    s_opp, s_up, s_dn, r_opp0, r_opp1, r_up, r_dn,
    m_opp, m_up, m_dn, n_opp0, n_opp1, n_up, n_dn,
    acc, t_opp, t_up, t_dn, w_opp0, w_opp1, w_up, w_dn,
    e_opp, e_up, e_dn, f_opp0, f_opp1, f_up, f_dn,
    k_sem, q_sem, send, recv,
):
    ctx = lax.axis_index("ctx")
    core = ctx % 2
    u, v = place(core)
    up_u = {"ctx": chip_of(u + 1, v, core) * 2 + core}
    dn_u = {"ctx": chip_of(u + 3, v, core) * 2 + core}
    up_v = {"ctx": chip_of(u, v + 1, core) * 2 + core}
    dn_v = {"ctx": chip_of(u, v + 3, core) * 2 + core}
    order = (2, 1, 3, 0)

    barrier = pltpu.get_barrier_semaphore()
    for device in (up_u, dn_u, up_v, dn_v):
        pl.semaphore_signal(barrier, inc=1, device_id=device, device_id_type=MESH)

    def k_copy(w):
        at = pl.ds(pl.multiple_of((w % 4) * 256, 256), 256)
        return pltpu.make_async_copy(kall.at[w // 4, :, at], kext.at[w, pl.ds(0, 576), :], k_sem.at[w])

    def q_copies(chunk):
        return [
            pltpu.make_async_copy(
                qall.at[chip_of(u + order[chunk], v + order[j], core)],
                qbuf.at[chunk % 2, j],
                q_sem.at[chunk % 2, j],
            )
            for j in range(4)
        ]

    def start_k(w, carry):
        k_copy(w).start()
        return carry

    lax.fori_loop(0, 32, start_k, 0)
    for copy in q_copies(0):
        copy.start()

    ones = jnp.where(lax.broadcasted_iota(jnp.int32, (64, 256), 0) == 0, 1.0, 0.0).astype(BF16)

    def set_ones(w, carry):
        kext[w, pl.ds(576, 64), :] = ones
        return carry

    lax.fori_loop(0, 32, set_ones, 0)
    pl.semaphore_wait(barrier, 4)

    sent = []

    def put(k, src, dst, device):
        copy = remote(src, dst, send.at[k], recv.at[k], device)
        copy.start()
        sent.append(copy)

    def get(k, ref):
        remote(ref, ref, send.at[k], recv.at[k], up_u).wait_recv()

    lane = lax.broadcasted_iota(jnp.int32, (128, 128), 1)

    def column(ref, at):
        return jnp.sum(jnp.where(lane == at, ref[...], 0.0), axis=1, keepdims=True)

    def keep(ref, at, peak, total):
        ref[...] = jnp.where(lane == at, peak, jnp.where(lane == at + 1, total, ref[...]))

    def flip_in(slot, ref):
        rows = ref.shape[0]
        full = jnp.concatenate([ref[...], jnp.zeros((128 - rows, 128), F32)], axis=0)
        mlin[slot] = full.T

    def joined(one, two):
        sums1, peak1, total1 = one
        sums2, peak2, total2 = two
        peak = jnp.maximum(peak1, peak2)
        f1, f2 = jnp.exp(peak1 - peak), jnp.exp(peak2 - peak)
        return sums1 * f1 + sums2.astype(F32) * f2, peak, total1 * f1 + total2 * f2

    def gather_tokens(chunk):
        for j in range(4):
            t = tall[chip_of(u + order[chunk], v + order[j], core)].astype(F32)
            for r in range(4):
                moved = t if r == 0 else pltpu.roll(t, 128 - r * 32, axis=1)
                picks[pl.ds((j * 4 + r) * 16, 16), :] = moved
        wide = lax.broadcasted_iota(jnp.int32, (256, 128), 1)
        token = (lax.broadcasted_iota(jnp.int32, (256, 256), 1) + 1).astype(F32)

        def one_window(w, carry):
            if chunk == 0:
                k_copy(w).wait()
            want = jnp.sum(jnp.where(wide == w, picks[...], 0.0), axis=1, keepdims=True)
            onehot = jnp.where(token == want, 1.0, 0.0).astype(BF16)
            rows = lax.dot_general(onehot, kext[w], NT, preferred_element_type=F32)
            at = pl.ds(pl.multiple_of(w * 16, 16), 16)
            ksel[:, at, :] = rows.astype(BF16).reshape(16, 16, 640)
            return carry

        lax.fori_loop(0, 32, one_window, 0)

    probe = jnp.where(lax.broadcasted_iota(jnp.int32, (16, 128), 1) == 64, 1.0, 0.0).astype(BF16)

    def attend_row(slot, j, r):
        row = j * 4 + r
        latent = ksel[row, :, 0:512]
        rope = qbuf[slot, j, :, 2048 + r * 64 : 2048 + (r + 1) * 64]
        rope = jnp.concatenate([rope, jnp.zeros((128, 64), BF16)], axis=1)
        rope = jnp.concatenate([rope, probe], axis=0)
        query = qbuf[slot, j, :, r * 512 : (r + 1) * 512]
        extra = lax.dot_general(rope, ksel[row, :, 512:640], NT, preferred_element_type=F32)
        scores = lax.dot_general(query, latent, NT, preferred_element_type=F32)
        scores = (scores + extra[0:128]) * SCALE
        scores = jnp.where(extra[128:129] > 0.5, scores, NONE)
        peak = jnp.maximum(jnp.max(scores, axis=1, keepdims=True), FLOOR)
        weights = jnp.exp(scores - peak).astype(BF16)
        total = jnp.sum(weights.astype(F32), axis=1, keepdims=True)
        sums = jnp.dot(weights, latent, preferred_element_type=F32)
        return sums, peak, total

    def half_chunk(chunk, half, put_row, merges):
        def one_block(j, carry):
            for r2 in range(2):
                got = attend_row(chunk % 2, j, half * 2 + r2)
                for slot, ref in merges:
                    at = j * 4 + r2 * 2
                    got = joined(got, (ref[j, r2], column(mlin.at[slot], at), column(mlin.at[slot], at + 1)))
                put_row(j, r2, *got)
            return carry

        lax.fori_loop(0, 4, one_block, 0)

    def send_half(chunk, half, sums_ref, ml_ref, merges):
        def put_row(j, r2, sums, peak, total):
            sums_ref[half, j, r2] = sums.astype(BF16)
            keep(mlcol, j * 4 + r2 * 2, peak, total)

        half_chunk(chunk, half, put_row, merges)
        ml_ref[half] = mlcol[...].T[0:16]

    mlcol[...] = jnp.zeros((128, 128), F32)

    def next_chunk(chunk):
        for copy in q_copies(chunk):
            copy.wait()
        if chunk < 3:
            for copy in q_copies(chunk + 1):
                copy.start()
        gather_tokens(chunk)

    next_chunk(0)
    send_half(0, 0, s_opp, m_opp, ())
    put(0, s_opp.at[0], r_opp0, up_u)
    put(1, m_opp.at[0], n_opp0, up_u)
    send_half(0, 1, s_opp, m_opp, ())
    put(2, s_opp.at[1], r_opp1, dn_u)
    put(3, m_opp.at[1], n_opp1, dn_u)

    next_chunk(1)
    send_half(1, 1, s_up, m_up, ())
    put(4, s_up.at[1], r_up.at[1], up_u)
    put(5, m_up.at[1], n_up.at[1], up_u)
    get(0, r_opp0)
    get(1, n_opp0)
    flip_in(0, n_opp0)
    send_half(1, 0, s_up, m_up, ((0, r_opp0),))
    put(6, s_up.at[0], r_up.at[0], up_u)
    put(7, m_up.at[0], n_up.at[0], up_u)

    next_chunk(2)
    send_half(2, 0, s_dn, m_dn, ())
    put(8, s_dn.at[0], r_dn.at[0], dn_u)
    put(9, m_dn.at[0], n_dn.at[0], dn_u)
    get(2, r_opp1)
    get(3, n_opp1)
    flip_in(0, n_opp1)
    send_half(2, 1, s_dn, m_dn, ((0, r_opp1),))
    put(10, s_dn.at[1], r_dn.at[1], dn_u)
    put(11, m_dn.at[1], n_dn.at[1], dn_u)

    next_chunk(3)
    for half in range(2):

        def put_row(j, r2, sums, peak, total):
            acc[j, half * 2 + r2] = sums
            keep(mlcol, j * 8 + half * 4 + r2 * 2, peak, total)

        half_chunk(3, half, put_row, ())

    for half in range(2):
        get(4 if half else 6, r_up.at[half])
        get(5 if half else 7, n_up.at[half])
        get(10 if half else 8, r_dn.at[half])
        get(11 if half else 9, n_dn.at[half])
        flip_in(half * 2, n_up.at[half])
        flip_in(half * 2 + 1, n_dn.at[half])

    def add_first(j, carry):
        for r in range(4):
            half, r2 = r // 2, r % 2
            at, here = j * 4 + r2 * 2, j * 8 + r * 2
            got = (acc[j, r], column(mlcol, here), column(mlcol, here + 1))
            for slot, ref in ((half * 2, r_up), (half * 2 + 1, r_dn)):
                got = joined(got, (ref[half, j, r2], column(mlin.at[slot], at), column(mlin.at[slot], at + 1)))
            acc[j, r] = got[0]
            keep(mlcol, here, got[1], got[2])
        return carry

    lax.fori_loop(0, 4, add_first, 0)

    def second_send(j, half, sums_ref, ml_ref, merge=None):
        if merge is not None:
            flip_in(0, merge[1])
        for r2 in range(2):
            r = half * 2 + r2
            at = j * 8 + r * 2
            got = (acc[j, r], column(mlcol, at), column(mlcol, at + 1))
            if merge is not None:
                got = joined(
                    got, (merge[0][r2], column(mlin.at[0], at % 8), column(mlin.at[0], at % 8 + 1))
                )
                keep(mlcol, at, got[1], got[2])
            sums_ref[half, r2] = got[0].astype(BF16)
        ml_ref[half] = mlcol[...].T[j * 8 : j * 8 + 8]

    second_send(0, 0, t_opp, e_opp)
    put(12, t_opp.at[0], w_opp0, up_v)
    put(13, e_opp.at[0], f_opp0, up_v)
    second_send(0, 1, t_opp, e_opp)
    put(14, t_opp.at[1], w_opp1, dn_v)
    put(15, e_opp.at[1], f_opp1, dn_v)
    second_send(1, 1, t_up, e_up)
    put(16, t_up.at[1], w_up.at[1], up_v)
    put(17, e_up.at[1], f_up.at[1], up_v)
    second_send(2, 0, t_dn, e_dn)
    put(20, t_dn.at[0], w_dn.at[0], dn_v)
    put(21, e_dn.at[0], f_dn.at[0], dn_v)
    get(12, w_opp0)
    get(13, f_opp0)
    second_send(1, 0, t_up, e_up, (w_opp0, f_opp0))
    put(18, t_up.at[0], w_up.at[0], up_v)
    put(19, e_up.at[0], f_up.at[0], up_v)
    get(14, w_opp1)
    get(15, f_opp1)
    second_send(2, 1, t_dn, e_dn, (w_opp1, f_opp1))
    put(22, t_dn.at[1], w_dn.at[1], dn_v)
    put(23, e_dn.at[1], f_dn.at[1], dn_v)

    for half in (1, 0):
        get(16 if half else 18, w_up.at[half])
        get(17 if half else 19, f_up.at[half])
        get(22 if half else 20, w_dn.at[half])
        get(23 if half else 21, f_dn.at[half])
        flip_in(half * 2, f_up.at[half])
        flip_in(half * 2 + 1, f_dn.at[half])
    for r in range(4):
        half, r2 = r // 2, r % 2
        at = 24 + r * 2
        got = (acc[3, r], column(mlcol, at), column(mlcol, at + 1))
        for slot, ref in ((half * 2, w_up), (half * 2 + 1, w_dn)):
            got = joined(got, (ref[half, r2], column(mlin.at[slot], r * 2), column(mlin.at[slot], r * 2 + 1)))
        out_ref[r] = (got[0] / got[2]).astype(BF16)
    for copy in sent:
        copy.wait_send()


def vmem():
    return pl.BlockSpec(memory_space=pltpu.VMEM)


def anywhere():
    return pl.BlockSpec(memory_space=pl.ANY)


def body(latent_cache, index_keys, query_latent, index_query, index_gates, selected):
    rows, heads, width = query_latent.shape
    tokens = latent_cache.shape[0]
    kt = latent_cache.T
    q_latent = query_latent[:, :, :LATENT].transpose(1, 0, 2).reshape(heads, rows * LATENT)
    q_rope = query_latent[:, :, LATENT:].transpose(1, 0, 2).reshape(heads, rows * (width - LATENT))
    qw = jnp.concatenate([q_latent, q_rope], axis=1)
    gates = jnp.pad(index_gates.T, ((0, 0), (0, 128 - rows)))
    iqg = jnp.concatenate([index_query.reshape(-1, 128), gates], axis=0)
    sel = selected.reshape(rows * 4, -1)
    dma = pltpu.SemaphoreType.DMA

    qall, kall, tall, index_scores = pl.pallas_call(
        gather_kernel,
        out_shape=(
            jax.ShapeDtypeStruct((16,) + qw.shape, BF16),
            jax.ShapeDtypeStruct((8, width, tokens), BF16),
            jax.ShapeDtypeStruct((16, 16, 128), BF16),
            jax.ShapeDtypeStruct((rows * 32, index_keys.shape[0]), F32),
        ),
        in_specs=[vmem()] * 5,
        out_specs=(anywhere(), anywhere(), anywhere(), vmem()),
        scratch_shapes=[
            pltpu.VMEM((16, 2) + iqg.shape, BF16),
            pltpu.VMEM((16, 16, 128), BF16),
            pltpu.VMEM((512, 128), F32),
            dma((20,)), dma((20,)), dma((20,)), dma((20,)), dma((21,)), dma((21,)),
            dma((9,)), dma((9,)), dma((16,)), dma((16,)), dma((4,)),
        ],
        compiler_params=pltpu.CompilerParams(
            collective_id=0, has_side_effects=True, vmem_limit_bytes=48 * 1024 * 1024
        ),
        name="gather",
    )(qw, kt, iqg, index_keys, sel)

    half = (4, 2, heads, LATENT)
    quarter = (2, heads, LATENT)
    attended = pl.pallas_call(
        attend_kernel,
        out_shape=jax.ShapeDtypeStruct((rows, heads, LATENT), BF16),
        in_specs=[anywhere(), anywhere(), vmem()],
        out_specs=vmem(),
        scratch_shapes=[
            pltpu.VMEM((32, 640, 256), BF16),
            pltpu.VMEM((16, 512, 640), BF16),
            pltpu.VMEM((2, 4) + qw.shape, BF16),
            pltpu.VMEM((256, 128), F32),
            pltpu.VMEM((128, 128), F32),
            pltpu.VMEM((4, 128, 128), F32),
        ]
        + [pltpu.VMEM((2,) + half, BF16)] * 3
        + [pltpu.VMEM(half, BF16)] * 2
        + [pltpu.VMEM((2,) + half, BF16)] * 2
        + [pltpu.VMEM((2, 16, 128), F32)] * 3
        + [pltpu.VMEM((16, 128), F32)] * 2
        + [pltpu.VMEM((2, 16, 128), F32)] * 2
        + [pltpu.VMEM((4, rows, heads, LATENT), F32)]
        + [pltpu.VMEM((2,) + quarter, BF16)] * 3
        + [pltpu.VMEM(quarter, BF16)] * 2
        + [pltpu.VMEM((2,) + quarter, BF16)] * 2
        + [pltpu.VMEM((2, 8, 128), F32)] * 3
        + [pltpu.VMEM((8, 128), F32)] * 2
        + [pltpu.VMEM((2, 8, 128), F32)] * 2
        + [dma((32,)), dma((2, 4)), dma((24,)), dma((24,))],
        compiler_params=pltpu.CompilerParams(
            collective_id=1, has_side_effects=True, vmem_limit_bytes=60 * 1024 * 1024
        ),
        name="attend",
    )(qall, kall, tall)
    return attended, index_scores


def solution(mesh):
    return jax.shard_map(
        body,
        mesh=mesh,
        in_specs=(
            P(("ctx", "row"), None),
            P("ctx", None),
            P(("row", "ctx"), None, None),
            P(("row", "ctx"), None, None),
            P(("row", "ctx"), None),
            P(("row", "ctx"), None),
        ),
        out_specs=(P(("row", "ctx"), None, None), P("row", "ctx")),
        check_vma=False,
    )
```

time: 754 us -> 190 us (0.25)
  waiting for transfers between devices: 270 us -> 0 us
  Pallas kernels: 0 us -> 179 us
  other arithmetic: 173 us -> 0.89 us
  local copies, waits for them, and re-layouts: 163 us -> 8.95 us
  matrix products: 102 us -> 0 us
  blocking collectives: 22.5 us -> 0 us
  between operations: 14.9 us -> 0.71 us
    pallas_call x0 -> x2, Pallas kernels: none -> 179 us  [the longest x1 102 us: body(): pl.pallas_call(attend_kernel, out_shape=jax.ShapeDtypeStruct((rows, heads...]
    reduce_scatter x1 -> x0, waiting for transfers between devices: 168 us -> none  [body(): lax.psum_scatter(sums, 'ctx', scatter_dimension=0, tiled=True)]
    reduce_max x128 -> x0, other arithmetic: 155 us -> none  [one_row(): return jnp.max(jnp.where(hit, what[:, None], -1), axis=0)]
    dot_general x19 -> x0, matrix products: 102 us -> none  [the longest x1 32.7 us: combine(): jnp.einsum('ghs,gsd->ghd', weights, keys[:, :, :LATENT], preferred_elemen...]
    slice x2, local copies, waits for them, and re-layouts: 67.9 us -> 1.93 us  [the longest x1 1.08 us: body(): query_latent[:, :, :LATENT].transpose(1, 0, 2).reshape(heads, rows * LATENT)]
    convert_element_type x1 -> x0, local copies, waits for them, and re-layouts: 51.8 us -> none  [pick_rows(): return rows_out.astype(jnp.bfloat16)]
    all_gather x4 -> x0, waiting for transfers between devices: 45.3 us -> none  [the longest x1 45.2 us: body(): picks = lax.all_gather(selected, 'ctx', axis=0, tiled=True)]
    unnamed x8 -> x0, waiting for transfers between devices: 29.2 us -> none
  transfers between devices with their start and end apart: 7 -> 0, of which waited for: 4 -> 0; matrix products, arithmetic and copies ran while one was open for 54% -> 0% of each run, Pallas kernels for 0% -> 0%
where the time goes in v1:
time: 190 us
  Pallas kernels  179 us (94%)
  local copies, waits for them, and re-layouts  8.95 us (5%)
    pallas_call x1, Pallas kernels, body(): pl.pallas_call(attend_kernel, out_shape=jax.ShapeDtypeStruct((rows, heads...  102 us
    pallas_call x1, Pallas kernels, body(): pl.pallas_call(gather_kernel, out_shape=(jax.ShapeDtypeStruct((16,) + qw....  77 us
    unnamed x9, local copies, waits for them, and re-layouts  5.92 us

profile of v1, /device:TPU:6, one launch (start us, length us, event | category | flops | bytes accessed | tf_op | source)
XLA Modules:
  0.0 189.6 jit_solution(17393488794976553361)
XLA Ops:
  0.6 0.0 copy-start
  0.6 0.9 copy.13
  1.5 0.8 reshape.19.sel_ref
  2.3 0.9 fusion.1.iq_ref
  3.2 0.9 slice.7
  4.0 0.1 copy.12
  4.1 1.1 slice.6
  5.2 0.2 copy.14
  5.5 0.0 copy-done
  5.5 0.0 copy-start.1
  5.5 1.2 copy-done.1
  6.7 77.0 %gather.1 = (bf16[16,128,2304]{2,1,0:T(8,128)(2,1)}, bf16[8,576,1024]{2,1,0:T(8,128)(2,1)}, bf16[16,16,128]{2,1,0:T(8,128)(2,1)S(1)}, f32[128,4096]{1,0:T(8,128)S(1)}) custom-call(bf16[128,2304]{1,0:T(8,128)(2,1)S(1)} %pad_maximum_fusion.q_ref, bf16[576,1024]{1,0:T(8,128)(2,1)S(1)} %bitcast.9, bf16[320,128]{1,0:T(8,128)(2,1)S(1)} %fusion.1.iq_ref, ...), custom_call_target="tpu_custom_call" | custom-call | tf_op jit(solution)/shard_map/gather/pallas_call | solution.py:584
  83.7 0.0 copy-start.2
  83.7 0.6 copy-done.2
  84.3 102.0 %attend.1 = bf16[4,128,512]{2,1,0:T(8,128)(2,1)} custom-call(bf16[16,128,2304]{2,1,0:T(8,128)(2,1)} %get-tuple-element.6.qall, bf16[8,576,1024]{2,1,0:T(8,128)(2,1)} %get-tuple-element.7.kall, bf16[16,16,128]{2,1,0:T(8,128)(2,1)} %copy-done.2), custom_call_target="tpu_custom_call" | custom-call | tf_op jit(solution)/shard_map/attend/pallas_call | solution.py:609
  186.4 1.9 copy.17
  188.3 1.3 copy.18
  (1 shorter events, 0.0 us)
Async XLA Ops:
  0.6 4.8 %copy-start = (bf16[1024,576]{0,1:T(8,128)(2,1)S(1)}, bf16[1024,576]{0,1:T(8,128)(2,1)}, u32[]{:S(2)}) copy-start(bf16[1024,576]{0,1:T(8,128)(2,1)} %param.6) | copy-start | bytes 3538948
  5.5 1.2 copy-start.1
  83.7 0.6 copy-start.2

commit v2 on v1

--- a/solution.py
+++ b/solution.py
@@ -1,3 +1,5 @@
+import math
+
 import jax
 import jax.numpy as jnp
 from jax import lax
@@ -7,7 +9,7 @@
 
 MESH = pl.DeviceIdType.MESH
 LATENT = 512
-SCALE = 192 ** (-0.5)
+TO_LOG2 = 192 ** (-0.5) * math.log2(math.e)
 NONE = -1e30
 FLOOR = -1e29
 F32 = jnp.float32
@@ -102,16 +104,19 @@
 
 
 def gather_kernel(
-    q_ref, k_ref, iq_ref, keys_ref, sel_ref,
+    q_ref, k_ref, iq_ref, keys_hbm, sel_ref,
     qall, kall, tall, isc_ref,
-    iqall, tsend, gate_ref,
+    iqall, tsend, gate_ref, keys_ref, logit_ref,
     q_send, q_recv, i_send, i_recv, p_send, p_recv, k_send, k_recv, t_send, t_recv, local,
 ):
     ctx, z = lax.axis_index("ctx"), lax.axis_index("row")
     core, chip = ctx % 2, ctx // 2
     other = 1 - core
     partner = {"ctx": chip * 2 + other}
-
+    x, y = chip // 4, chip % 4
+
+    keys_copy = pltpu.make_async_copy(keys_hbm, keys_ref, local.at[4])
+    keys_copy.start()
     barrier = pltpu.get_barrier_semaphore()
     for step in range(1, 16):
         pl.semaphore_signal(
@@ -120,25 +125,6 @@
     pl.semaphore_signal(barrier, inc=1, device_id=partner, device_id_type=MESH)
     for step in (1, 3):
         pl.semaphore_signal(barrier, inc=1, device_id={"row": (z + step) % 4}, device_id_type=MESH)
-
-    def add_picks(i, total):
-        token = sel_ref[pl.ds(i, 1), :]
-        to = (token >> 13) * 16 + ((token >> 4) & 15)
-        window = (i // 4) * 32 + ((token >> 8) & 31)
-        value = ((token & 255) + 1).astype(F32)
-        width = token.shape[1]
-        left = lax.broadcasted_iota(jnp.int32, (256, width), 0) == to
-        right = lax.broadcasted_iota(jnp.int32, (128, width), 0) == window
-        return total + lax.dot_general(
-            jnp.where(left, 1.0, 0.0).astype(BF16),
-            jnp.where(right, value, 0.0).astype(BF16),
-            NT,
-            preferred_element_type=F32,
-        )
-
-    table = lax.fori_loop(0, sel_ref.shape[0], add_picks, jnp.zeros((256, 128), F32))
-    tsend[...] = table.astype(BF16).reshape(16, 16, 128)
-
     pl.semaphore_wait(barrier, 18)
 
     to_partner = []
@@ -157,15 +143,6 @@
     copy.start()
     to_partner.append(copy)
 
-    table_copies = []
-    for step in range(1, 16):
-        to = (chip + step) % 16
-        copy = remote(
-            tsend.at[to], tall.at[chip], t_send.at[step], t_recv.at[step], {"ctx": to * 2 + core}
-        )
-        copy.start()
-        table_copies.append(copy)
-
     k_rows = k_ref.shape[0]
     parts = (pl.ds(0, k_rows), pl.ds(0, k_rows // 2), pl.ds(k_rows // 2, k_rows // 2))
     k_sent = []
@@ -183,94 +160,163 @@
         remote(ref, ref, k_send.at[k], k_recv.at[k], {"row": z}).wait_recv()
 
     up, down = {"row": (z + 1) % 4}, {"row": (z + 3) % 4}
+    query_ring = Ring(q_ref, lambda p, rows: qall.at[p, rows], q_ref.shape[0], q_send, q_recv, core)
+    query_ring.start()
     k_put(0, k_ref, k_view(z, 0), up)
     k_put(1, k_ref, k_view(z, 0), down)
     k_put(4, k_ref, k_view(z, 0), partner)
 
-    query_ring = Ring(q_ref, lambda p, rows: qall.at[p, rows], q_ref.shape[0], q_send, q_recv, core)
-    query_ring.start()
-
     own = [
+        pltpu.make_async_copy(iq_ref, iqall.at[chip, core], local.at[3]),
         pltpu.make_async_copy(q_ref, qall.at[chip], local.at[0]),
         pltpu.make_async_copy(k_ref, k_view(z, 0), local.at[1]),
-        pltpu.make_async_copy(tsend.at[chip], tall.at[chip], local.at[2]),
-        pltpu.make_async_copy(iq_ref, iqall.at[chip, core], local.at[3]),
     ]
     for copy in own:
         copy.start()
 
+    pieces = sel_ref.shape[1] // 512
+
+    def add_picks(i, total):
+        at = pl.ds(pl.multiple_of((i % pieces) * 512, 512), 512)
+        token = sel_ref[pl.ds(i // pieces, 1), at]
+        to = (token >> 13) * 16 + ((token >> 4) & 15)
+        window = (i // pieces) * 32 + ((token >> 8) & 31)
+        value = ((token & 255) + 1).astype(F32)
+        left = lax.broadcasted_iota(jnp.int32, (256, 512), 0) == to
+        right = lax.broadcasted_iota(jnp.int32, (128, 512), 0) == window
+        return total + lax.dot_general(
+            jnp.where(left, 1.0, 0.0).astype(BF16),
+            jnp.where(right, value, 0.0).astype(BF16),
+            NT,
+            preferred_element_type=F32,
+        )
+
+    table = lax.fori_loop(0, sel_ref.shape[0] * pieces, add_picks, jnp.zeros((256, 128), F32))
+    tsend[...] = table.astype(BF16).reshape(16, 16, 128)
+
+    table_copies = []
+
+    def send_tables():
+        for step in range(1, 16):
+            to = (chip + step) % 16
+            copy = remote(
+                tsend.at[to], tall.at[chip], t_send.at[step], t_recv.at[step], {"ctx": to * 2 + core}
+            )
+            copy.start()
+            table_copies.append(copy)
+        own.append(pltpu.make_async_copy(tsend.at[chip], tall.at[chip], local.at[2]))
+        own[-1].start()
+
+    oa, ob = place(other)
+    columns = (0, 3, 1, 2)
+
+    def wait_partner(da, db):
+        if db:
+            j = columns.index(da)
+            events = {3: ((5 + 4 * j, 0),), 1: ((6 + 4 * j, 0),), 2: ((7 + 4 * j, 1), (8 + 4 * j, 2))}[db]
+        else:
+            events = {0: ((0, 0),), 3: ((1, 0),), 1: ((2, 0),), 2: ((3, 1), (4, 2))}[da]
+        for event, part in events:
+            ref = iqall.at[chip_of(oa + da, ob + db, other), other, index_ring.halves[part]]
+            remote(ref, ref, p_send.at[event], p_recv.at[event], partner).wait_recv()
+
+    tile = 512
+    tiles = keys_ref.shape[0] // tile
+
+    def index_chip(p):
+        for c in range(2):
+            gates = iqall[p, c, 256:320, :].astype(F32)
+            for r in range(4):
+                gate_ref[pl.ds((c * 4 + r) * 64, 64), :] = jnp.broadcast_to(gates[:, r : r + 1], (64, 128))
+
+        def token_tile(t):
+            return pl.ds(pl.multiple_of(t * tile, tile), tile)
+
+        def logits(t, slot):
+            logit_ref[slot] = lax.dot_general(
+                iqall[p, :, 0:256, :].reshape(512, 128), keys_ref[token_tile(t), :], NT, preferred_element_type=F32
+            )
+
+        def gated_sum(t, slot):
+            columns = []
+            for lanes in range(0, tile, 128):
+                rows = []
+                for i in range(8):
+                    total = None
+                    for h in range(0, 64, 8):
+                        part = logit_ref[slot, i * 64 + h : i * 64 + h + 8, lanes : lanes + 128]
+                        part = jnp.maximum(part, 0.0) * gate_ref[i * 64 + h : i * 64 + h + 8, :]
+                        total = part if total is None else total + part
+                    rows.append(jnp.sum(total, axis=0, keepdims=True))
+                columns.append(jnp.concatenate(rows, axis=0))
+            isc_ref[pl.ds(pl.multiple_of(p * 8, 8), 8), token_tile(t)] = jnp.concatenate(columns, axis=1)
+
+        logits(0, 0)
+
+        def two_tiles(i, carry):
+            logits(i * 2 + 1, 1)
+            gated_sum(i * 2, 0)
+            logits(jnp.minimum(i * 2 + 2, tiles - 1), 0)
+            gated_sum(i * 2 + 1, 1)
+            return carry
+
+        lax.fori_loop(0, tiles // 2, two_tiles, 0)
+
+    def index_chips(low, high, dx, dy):
+        def one(k, carry):
+            index_chip((x + dx(k)) % 4 * 4 + (y + dy(k)) % 4)
+            return carry
+
+        lax.fori_loop(low, high, one, 0)
+
+    beside = (lambda k: (1 - k // 2) * (1 + 2 * (k % 2)), lambda k: (k // 2) * (1 + 2 * (k % 2)))
+    corner = (lambda k: 1 + 2 * (k % 2), lambda k: 1 + 2 * (k // 2))
+    rest = (
+        lambda k: 2 * (k == 0) + 2 * (k == 2) + 2 * (k == 3) + (k == 4) + 3 * (k == 5) + 2 * (k == 6),
+        lambda k: 2 * (k == 1) + (k == 2) + 3 * (k == 3) + 2 * (k == 4) + 2 * (k == 5) + 2 * (k == 6),
+    )
+
     index_ring.near()
+    send_tables()
     index_ring.relay(0)
     index_ring.far()
+    own[0].wait()
+    keys_copy.wait()
+    wait_partner(0, 0)
+    index_chips(0, 1, lambda k: k, lambda k: k)
     index_ring.relay(1)
     index_ring.relay(2)
     index_ring.last(0)
     index_ring.relay(3)
     for j in (1, 2, 3):
         index_ring.last(j)
-
-    oa, ob = place(other)
-    columns = (oa, oa + 3, oa + 1, oa + 2)
-    arrivals = [(0, (oa, ob), 0), (1, (oa + 3, ob), 0), (2, (oa + 1, ob), 0), (3, (oa + 2, ob), 1), (4, (oa + 2, ob), 2)]
-    for j in range(4):
-        column = columns[j]
-        arrivals += [
-            (5 + 4 * j, (column, ob + 3), 0),
-            (6 + 4 * j, (column, ob + 1), 0),
-            (7 + 4 * j, (column, ob + 2), 1),
-            (8 + 4 * j, (column, ob + 2), 2),
-        ]
-    for event, block, part in arrivals:
-        ref = iqall.at[chip_of(*block, other), other, index_ring.halves[part]]
-        remote(ref, ref, p_send.at[event], p_recv.at[event], partner).wait_recv()
-    own[3].wait()
-
-    tile = 512
-
-    def index_chip(p, carry):
-        for c in range(2):
-            gates = iqall[p, c, 256:320, :].astype(F32)
-            for r in range(4):
-                gate_ref[pl.ds((c * 4 + r) * 64, 64), :] = jnp.broadcast_to(gates[:, r : r + 1], (64, 128))
-        queries = iqall[p, :, 0:256, :].reshape(512, 128)
-
-        def some_tokens(t, carry):
-            at = pl.ds(pl.multiple_of(t * tile, tile), tile)
-            logits = lax.dot_general(queries, keys_ref[at, :], NT, preferred_element_type=F32)
-            rows = []
-            for i in range(8):
-                gate = jnp.concatenate([gate_ref[pl.ds(i * 64, 64), :]] * (tile // 128), axis=1)
-                part = jnp.maximum(logits[i * 64 : (i + 1) * 64, :], 0.0) * gate
-                rows.append(jnp.sum(part, axis=0, keepdims=True))
-            isc_ref[pl.ds(pl.multiple_of(p * 8, 8), 8), at] = jnp.concatenate(rows, axis=0)
-            return carry
-
-        return lax.fori_loop(0, keys_ref.shape[0] // tile, some_tokens, carry)
-
-    def index_chips(low, high):
-        lax.fori_loop(low, high, index_chip, 0)
-
-    index_chips(0, 2)
     query_ring.near()
     query_ring.relay(0)
-    index_chips(2, 6)
+    for da, db in ((3, 0), (1, 0), (0, 3), (0, 1)):
+        wait_partner(da, db)
+    index_chips(0, 4, *beside)
+    query_ring.far()
     k_get(0, z + 3, 0)
     k_put(2, k_view(z + 3, 1), k_view(z + 3, 1), up)
     k_put(5, k_view(z + 3, 0), k_view(z + 3, 0), partner)
     k_get(1, z + 1, 0)
     k_put(3, k_view(z + 1, 2), k_view(z + 1, 2), down)
     k_put(6, k_view(z + 1, 0), k_view(z + 1, 0), partner)
-    query_ring.far()
-    index_chips(6, 9)
+    for da, db in ((3, 3), (3, 1), (1, 3), (1, 1)):
+        wait_partner(da, db)
+    index_chips(0, 2, *corner)
     query_ring.relay(1)
     query_ring.relay(2)
-    index_chips(9, 13)
+    index_chips(2, 4, *corner)
+    for da, db in ((2, 0), (0, 2), (3, 2), (1, 2), (2, 3), (2, 1), (2, 2)):
+        wait_partner(da, db)
+    index_chips(0, 3, *rest)
+    query_ring.relay(3)
     k_get(2, z + 2, 1)
     k_put(7, k_view(z + 2, 1), k_view(z + 2, 1), partner)
     k_get(3, z + 2, 2)
     k_put(8, k_view(z + 2, 2), k_view(z + 2, 2), partner)
-    query_ring.relay(3)
-    index_chips(13, 16)
+    index_chips(3, 7, *rest)
 
     for j in range(4):
         query_ring.last(j)
@@ -284,7 +330,7 @@
         remote(
             tall.at[frm], tall.at[frm], t_send.at[step], t_recv.at[step], partner
         ).wait_recv()
-    for copy in own[:3]:
+    for copy in own[1:]:
         copy.wait()
     query_ring.finish()
     index_ring.finish()
@@ -294,7 +340,7 @@
 
 def attend_kernel(
     qall, kall, tall, out_ref,
-    kext, ksel, qbuf, picks, mlcol, mlin,
+    kext, ksel, qbuf, rope, raw, picks, mlcol, mlin,
     s_opp, s_up, s_dn, r_opp0, r_opp1, r_up, r_dn,
     m_opp, m_up, m_dn, n_opp0, n_opp1, n_up, n_dn,
     acc, t_opp, t_up, t_dn, w_opp0, w_opp1, w_up, w_dn,
@@ -321,11 +367,14 @@
     def q_copies(chunk):
         return [
             pltpu.make_async_copy(
-                qall.at[chip_of(u + order[chunk], v + order[j], core)],
-                qbuf.at[chunk % 2, j],
-                q_sem.at[chunk % 2, j],
+                qall.at[chip_of(u + order[chunk], v + order[j], core), :, pl.ds(r * 512, width)],
+                qbuf.at[chunk % 2, j * 4 + r, pl.ds(0, 128), pl.ds(0, 512)]
+                if r < 4
+                else rope.at[chunk % 2, j],
+                q_sem.at[chunk % 2, j * 5 + r],
             )
             for j in range(4)
+            for r, width in ((0, 512), (1, 512), (2, 512), (3, 512), (4, 256))
         ]
 
     def start_k(w, carry):
@@ -343,6 +392,14 @@
         return carry
 
     lax.fori_loop(0, 32, set_ones, 0)
+    probe = jnp.where(lax.broadcasted_iota(jnp.int32, (16, 640), 1) == 576, 1.0, 0.0).astype(BF16)
+
+    def set_probe(row, carry):
+        for slot in range(2):
+            qbuf[slot, row, pl.ds(128, 16), :] = probe
+        return carry
+
+    lax.fori_loop(0, 16, set_probe, 0)
     pl.semaphore_wait(barrier, 4)
 
     sent = []
@@ -372,7 +429,7 @@
         sums1, peak1, total1 = one
         sums2, peak2, total2 = two
         peak = jnp.maximum(peak1, peak2)
-        f1, f2 = jnp.exp(peak1 - peak), jnp.exp(peak2 - peak)
+        f1, f2 = jnp.exp2((peak1 - peak) * TO_LOG2), jnp.exp2((peak2 - peak) * TO_LOG2)
         return sums1 * f1 + sums2.astype(F32) * f2, peak, total1 * f1 + total2 * f2
 
     def gather_tokens(chunk):
@@ -384,44 +441,58 @@
         wide = lax.broadcasted_iota(jnp.int32, (256, 128), 1)
         token = (lax.broadcasted_iota(jnp.int32, (256, 256), 1) + 1).astype(F32)
 
-        def one_window(w, carry):
-            if chunk == 0:
-                k_copy(w).wait()
-            want = jnp.sum(jnp.where(wide == w, picks[...], 0.0), axis=1, keepdims=True)
-            onehot = jnp.where(token == want, 1.0, 0.0).astype(BF16)
-            rows = lax.dot_general(onehot, kext[w], NT, preferred_element_type=F32)
-            at = pl.ds(pl.multiple_of(w * 16, 16), 16)
-            ksel[:, at, :] = rows.astype(BF16).reshape(16, 16, 640)
+        def some_windows(i, carry):
+            for step in range(4):
+                w = i * 4 + step
+                if chunk == 0:
+                    k_copy(w).wait()
+            for step in range(4):
+                w = i * 4 + step
+                want = jnp.sum(jnp.where(wide == w, picks[...], 0.0), axis=1, keepdims=True)
+                onehot = jnp.where(token == want, 1.0, 0.0).astype(BF16)
+                rows = lax.dot_general(onehot, kext[w], NT, preferred_element_type=F32)
+                at = pl.ds(pl.multiple_of(w * 16, 16), 16)
+                ksel[:, at, :] = rows.astype(BF16).reshape(16, 16, 640)
             return carry
 
-        lax.fori_loop(0, 32, one_window, 0)
-
-    probe = jnp.where(lax.broadcasted_iota(jnp.int32, (16, 128), 1) == 64, 1.0, 0.0).astype(BF16)
-
-    def attend_row(slot, j, r):
-        row = j * 4 + r
-        latent = ksel[row, :, 0:512]
-        rope = qbuf[slot, j, :, 2048 + r * 64 : 2048 + (r + 1) * 64]
-        rope = jnp.concatenate([rope, jnp.zeros((128, 64), BF16)], axis=1)
-        rope = jnp.concatenate([rope, probe], axis=0)
-        query = qbuf[slot, j, :, r * 512 : (r + 1) * 512]
-        extra = lax.dot_general(rope, ksel[row, :, 512:640], NT, preferred_element_type=F32)
-        scores = lax.dot_general(query, latent, NT, preferred_element_type=F32)
-        scores = (scores + extra[0:128]) * SCALE
-        scores = jnp.where(extra[128:129] > 0.5, scores, NONE)
+        lax.fori_loop(0, 8, some_windows, 0)
+
+    def set_rope(slot):
+        def one_block(j, carry):
+            for r in range(4):
+                part = rope[slot, j, :, r * 64 : (r + 1) * 64]
+                qbuf[slot, j * 4 + r, pl.ds(0, 128), pl.ds(512, 128)] = jnp.concatenate(
+                    [part, jnp.zeros((128, 64), BF16)], axis=1
+                )
+            return carry
+
+        lax.fori_loop(0, 4, one_block, 0)
+
+    def score_row(slot, row, to):
+        raw[to] = lax.dot_general(qbuf[slot, row], ksel[row], NT, preferred_element_type=F32)
+
+    def attend_row(row, frm):
+        scores = jnp.where(raw[frm, 128:129, :] > 0.5, raw[frm, 0:128, :], NONE)
         peak = jnp.maximum(jnp.max(scores, axis=1, keepdims=True), FLOOR)
-        weights = jnp.exp(scores - peak).astype(BF16)
-        total = jnp.sum(weights.astype(F32), axis=1, keepdims=True)
-        sums = jnp.dot(weights, latent, preferred_element_type=F32)
+        weights = jnp.exp2((scores - peak) * TO_LOG2)
+        total = jnp.sum(weights, axis=1, keepdims=True)
+        sums = jnp.dot(weights.astype(BF16), ksel[row, :, 0:512], preferred_element_type=F32)
         return sums, peak, total
 
     def half_chunk(chunk, half, put_row, merges):
+        slot = chunk % 2
+        score_row(slot, half * 2, 0)
+
         def one_block(j, carry):
             for r2 in range(2):
-                got = attend_row(chunk % 2, j, half * 2 + r2)
-                for slot, ref in merges:
+                row = j * 4 + half * 2 + r2
+                score_row(slot, (row + 1 if r2 == 0 else jnp.minimum(row + 3, 12 + half * 2)), 1 - r2)
+                got = attend_row(row, r2)
+                for at_slot, ref in merges:
                     at = j * 4 + r2 * 2
-                    got = joined(got, (ref[j, r2], column(mlin.at[slot], at), column(mlin.at[slot], at + 1)))
+                    got = joined(
+                        got, (ref[j, r2], column(mlin.at[at_slot], at), column(mlin.at[at_slot], at + 1))
+                    )
                 put_row(j, r2, *got)
             return carry
 
@@ -443,6 +514,7 @@
         if chunk < 3:
             for copy in q_copies(chunk + 1):
                 copy.start()
+        set_rope(chunk % 2)
         gather_tokens(chunk)
 
     next_chunk(0)
@@ -578,7 +650,6 @@
     qw = jnp.concatenate([q_latent, q_rope], axis=1)
     gates = jnp.pad(index_gates.T, ((0, 0), (0, 128 - rows)))
     iqg = jnp.concatenate([index_query.reshape(-1, 128), gates], axis=0)
-    sel = selected.reshape(rows * 4, -1)
     dma = pltpu.SemaphoreType.DMA
 
     qall, kall, tall, index_scores = pl.pallas_call(
@@ -589,20 +660,22 @@
             jax.ShapeDtypeStruct((16, 16, 128), BF16),
             jax.ShapeDtypeStruct((rows * 32, index_keys.shape[0]), F32),
         ),
-        in_specs=[vmem()] * 5,
+        in_specs=[vmem(), vmem(), vmem(), anywhere(), vmem()],
         out_specs=(anywhere(), anywhere(), anywhere(), vmem()),
         scratch_shapes=[
             pltpu.VMEM((16, 2) + iqg.shape, BF16),
             pltpu.VMEM((16, 16, 128), BF16),
             pltpu.VMEM((512, 128), F32),
+            pltpu.VMEM(index_keys.shape, BF16),
+            pltpu.VMEM((2, 512, 512), F32),
             dma((20,)), dma((20,)), dma((20,)), dma((20,)), dma((21,)), dma((21,)),
-            dma((9,)), dma((9,)), dma((16,)), dma((16,)), dma((4,)),
+            dma((9,)), dma((9,)), dma((16,)), dma((16,)), dma((5,)),
         ],
         compiler_params=pltpu.CompilerParams(
             collective_id=0, has_side_effects=True, vmem_limit_bytes=48 * 1024 * 1024
         ),
         name="gather",
-    )(qw, kt, iqg, index_keys, sel)
+    )(qw, kt, iqg, index_keys, selected)
 
     half = (4, 2, heads, LATENT)
     quarter = (2, heads, LATENT)
@@ -614,7 +687,9 @@
         scratch_shapes=[
             pltpu.VMEM((32, 640, 256), BF16),
             pltpu.VMEM((16, 512, 640), BF16),
-            pltpu.VMEM((2, 4) + qw.shape, BF16),
+            pltpu.VMEM((2, 16, 144, 640), BF16),
+            pltpu.VMEM((2, 4, heads, 256), BF16),
+            pltpu.VMEM((2, 144, 512), F32),
             pltpu.VMEM((256, 128), F32),
             pltpu.VMEM((128, 128), F32),
             pltpu.VMEM((4, 128, 128), F32),
@@ -632,7 +707,7 @@
         + [pltpu.VMEM((2, 8, 128), F32)] * 3
         + [pltpu.VMEM((8, 128), F32)] * 2
         + [pltpu.VMEM((2, 8, 128), F32)] * 2
-        + [dma((32,)), dma((2, 4)), dma((24,)), dma((24,))],
+        + [dma((32,)), dma((2, 20)), dma((24,)), dma((24,))],
         compiler_params=pltpu.CompilerParams(
             collective_id=1, has_side_effects=True, vmem_limit_bytes=60 * 1024 * 1024
         ),

time: 190 us -> 164 us (0.86)
  Pallas kernels: 179 us -> 154 us
    pallas_call x1, Pallas kernels: 102 us -> 85 us  [body(): pl.pallas_call(attend_kernel, out_shape=jax.ShapeDtypeStruct((rows, heads...]
    pallas_call x1, Pallas kernels: 77 us -> 69 us  [body(): pl.pallas_call(gather_kernel, out_shape=(jax.ShapeDtypeStruct((16,) + qw....]
    unnamed x9 -> x11, local copies, waits for them, and re-layouts: 5.92 us -> 5.92 us
where the time goes in v2:
time: 164 us
  Pallas kernels  154 us (94%)
  local copies, waits for them, and re-layouts  8.17 us (5%)
    pallas_call x1, Pallas kernels, body(): pl.pallas_call(attend_kernel, out_shape=jax.ShapeDtypeStruct((rows, heads...  85 us
    pallas_call x1, Pallas kernels, body(): pl.pallas_call(gather_kernel, out_shape=(jax.ShapeDtypeStruct((16,) + qw....  69 us
    unnamed x11, local copies, waits for them, and re-layouts  5.92 us

profile of v2, /device:TPU:6, one launch (start us, length us, event | category | flops | bytes accessed | tf_op | source)
XLA Modules:
  0.0 163.8 jit_solution(15649023290273548719)
XLA Ops:
  0.6 0.0 copy-start.3
  0.6 0.0 copy-start
  0.6 0.9 copy.13
  1.5 0.9 fusion.1.iq_ref
  2.4 0.9 slice.7
  3.2 0.1 copy.12
  3.4 1.1 slice.6
  4.4 0.2 copy.14
  4.7 0.0 copy-done.3
  4.7 0.0 copy-done
  4.7 0.0 copy-start.1
  4.7 1.2 copy-done.1
  6.0 69.0 %gather.1 = (bf16[16,128,2304]{2,1,0:T(8,128)(2,1)}, bf16[8,576,1024]{2,1,0:T(8,128)(2,1)}, bf16[16,16,128]{2,1,0:T(8,128)(2,1)S(1)}, f32[128,4096]{1,0:T(8,128)S(1)}) custom-call(bf16[128,2304]{1,0:T(8,128)(2,1)S(1)} %pad_maximum_fusion.q_ref, bf16[576,1024]{1,0:T(8,128)(2,1)S(1)} %bitcast.9, bf16[320,128]{1,0:T(8,128)(2,1)S(1)} %fusion.1.iq_ref, ...), custom_call_target="tpu_custom_call" | custom-call | tf_op jit(solution)/shard_map/gather/pallas_call | solution.py:655
  75.0 0.0 copy-start.2
  75.0 0.6 copy-done.2
  75.6 85.0 %attend.1 = bf16[4,128,512]{2,1,0:T(8,128)(2,1)} custom-call(bf16[16,128,2304]{2,1,0:T(8,128)(2,1)} %get-tuple-element.6.qall, bf16[8,576,1024]{2,1,0:T(8,128)(2,1)} %get-tuple-element.7.kall, bf16[16,16,128]{2,1,0:T(8,128)(2,1)} %copy-done.2), custom_call_target="tpu_custom_call" | custom-call | tf_op jit(solution)/shard_map/attend/pallas_call | solution.py:682
  160.6 1.9 %copy.17 = bf16[4,128,512]{2,1,0:T(8,128)(2,1)} copy(bf16[4,128,512]{2,1,0:T(8,128)(2,1)} %attend.1) | data formatting | bytes 1048576
  162.5 1.3 copy.18
  (1 shorter events, 0.0 us)
Async XLA Ops:
  0.6 4.1 %copy-start.3 = (s32[4,2048]{1,0:T(4,128)S(1)}, s32[4,2048]{1,0:T(4,128)}, u32[]{:S(2)}) copy-start(s32[4,2048]{1,0:T(4,128)} %sel_ref.1) | copy-start | bytes 98308
  0.6 4.1 %copy-start = (bf16[1024,576]{0,1:T(8,128)(2,1)S(1)}, bf16[1024,576]{0,1:T(8,128)(2,1)}, u32[]{:S(2)}) copy-start(bf16[1024,576]{0,1:T(8,128)(2,1)} %param.6) | copy-start | bytes 3538948
  4.7 1.2 copy-start.1
  75.0 0.6 copy-start.2

commit v3 on v2

--- a/solution.py
+++ b/solution.py
@@ -364,17 +364,24 @@
         at = pl.ds(pl.multiple_of((w % 4) * 256, 256), 256)
         return pltpu.make_async_copy(kall.at[w // 4, :, at], kext.at[w, pl.ds(0, 576), :], k_sem.at[w])
 
-    def q_copies(chunk):
+    groups = ((2, 2), (3, 1), (1, 3), (0, 0))
+
+    def q_copies(group):
+        copies = []
+        for j in range(4):
+            for half in range(2):
+                chip = chip_of(u + groups[group][half], v + order[j], core)
+                for r in (half * 2, half * 2 + 1):
+                    copies.append((
+                        qall.at[chip, :, pl.ds(r * 512, 512)],
+                        qbuf.at[group % 2, j * 4 + r, pl.ds(0, 128), pl.ds(0, 512)],
+                    ))
+                copies.append((
+                    qall.at[chip, :, pl.ds(2048 + half * 128, 128)],
+                    rope.at[group % 2, j, :, pl.ds(half * 128, 128)],
+                ))
         return [
-            pltpu.make_async_copy(
-                qall.at[chip_of(u + order[chunk], v + order[j], core), :, pl.ds(r * 512, width)],
-                qbuf.at[chunk % 2, j * 4 + r, pl.ds(0, 128), pl.ds(0, 512)]
-                if r < 4
-                else rope.at[chunk % 2, j],
-                q_sem.at[chunk % 2, j * 5 + r],
-            )
-            for j in range(4)
-            for r, width in ((0, 512), (1, 512), (2, 512), (3, 512), (4, 256))
+            pltpu.make_async_copy(src, dst, q_sem.at[group % 2, n]) for n, (src, dst) in enumerate(copies)
         ]
 
     def start_k(w, carry):
@@ -434,8 +441,8 @@
 
     def gather_tokens(chunk):
         for j in range(4):
-            t = tall[chip_of(u + order[chunk], v + order[j], core)].astype(F32)
             for r in range(4):
+                t = tall[chip_of(u + groups[chunk][r // 2], v + order[j], core)].astype(F32)
                 moved = t if r == 0 else pltpu.roll(t, 128 - r * 32, axis=1)
                 picks[pl.ds((j * 4 + r) * 16, 16), :] = moved
         wide = lax.broadcasted_iota(jnp.int32, (256, 128), 1)
@@ -529,17 +536,17 @@
     send_half(1, 1, s_up, m_up, ())
     put(4, s_up.at[1], r_up.at[1], up_u)
     put(5, m_up.at[1], n_up.at[1], up_u)
+    send_half(1, 0, s_dn, m_dn, ())
+    put(8, s_dn.at[0], r_dn.at[0], dn_u)
+    put(9, m_dn.at[0], n_dn.at[0], dn_u)
+
+    next_chunk(2)
     get(0, r_opp0)
     get(1, n_opp0)
     flip_in(0, n_opp0)
-    send_half(1, 0, s_up, m_up, ((0, r_opp0),))
+    send_half(2, 0, s_up, m_up, ((0, r_opp0),))
     put(6, s_up.at[0], r_up.at[0], up_u)
     put(7, m_up.at[0], n_up.at[0], up_u)
-
-    next_chunk(2)
-    send_half(2, 0, s_dn, m_dn, ())
-    put(8, s_dn.at[0], r_dn.at[0], dn_u)
-    put(9, m_dn.at[0], n_dn.at[0], dn_u)
     get(2, r_opp1)
     get(3, n_opp1)
     flip_in(0, n_opp1)
@@ -548,59 +555,61 @@
     put(11, m_dn.at[1], n_dn.at[1], dn_u)
 
     next_chunk(3)
-    for half in range(2):
+    for half, early, early_ml, k in ((0, r_dn, n_dn, 8), (1, r_up, n_up, 4)):
+        get(k, early.at[half])
+        get(k + 1, early_ml.at[half])
+        flip_in(0, early_ml.at[half])
 
         def put_row(j, r2, sums, peak, total):
             acc[j, half * 2 + r2] = sums
             keep(mlcol, j * 8 + half * 4 + r2 * 2, peak, total)
 
-        half_chunk(3, half, put_row, ())
-
-    for half in range(2):
-        get(4 if half else 6, r_up.at[half])
-        get(5 if half else 7, n_up.at[half])
-        get(10 if half else 8, r_dn.at[half])
-        get(11 if half else 9, n_dn.at[half])
-        flip_in(half * 2, n_up.at[half])
-        flip_in(half * 2 + 1, n_dn.at[half])
-
-    def add_first(j, carry):
+        half_chunk(3, half, put_row, ((0, early.at[half]),))
+
+    get(6, r_up.at[0])
+    get(7, n_up.at[0])
+    flip_in(0, n_up.at[0])
+    get(10, r_dn.at[1])
+    get(11, n_dn.at[1])
+    flip_in(1, n_dn.at[1])
+
+    def add_late(j):
         for r in range(4):
             half, r2 = r // 2, r % 2
             at, here = j * 4 + r2 * 2, j * 8 + r * 2
+            late = (r_up, r_dn)[half][half, j, r2]
             got = (acc[j, r], column(mlcol, here), column(mlcol, here + 1))
-            for slot, ref in ((half * 2, r_up), (half * 2 + 1, r_dn)):
-                got = joined(got, (ref[half, j, r2], column(mlin.at[slot], at), column(mlin.at[slot], at + 1)))
+            got = joined(got, (late, column(mlin.at[half], at), column(mlin.at[half], at + 1)))
             acc[j, r] = got[0]
             keep(mlcol, here, got[1], got[2])
-        return carry
-
-    lax.fori_loop(0, 4, add_first, 0)
 
     def second_send(j, half, sums_ref, ml_ref, merge=None):
         if merge is not None:
-            flip_in(0, merge[1])
+            flip_in(2, merge[1])
         for r2 in range(2):
             r = half * 2 + r2
             at = j * 8 + r * 2
+            if merge is None:
+                sums_ref[half, r2] = acc[j, r].astype(BF16)
+                continue
             got = (acc[j, r], column(mlcol, at), column(mlcol, at + 1))
-            if merge is not None:
-                got = joined(
-                    got, (merge[0][r2], column(mlin.at[0], at % 8), column(mlin.at[0], at % 8 + 1))
-                )
-                keep(mlcol, at, got[1], got[2])
+            got = joined(got, (merge[0][r2], column(mlin.at[2], at % 8), column(mlin.at[2], at % 8 + 1)))
+            keep(mlcol, at, got[1], got[2])
             sums_ref[half, r2] = got[0].astype(BF16)
         ml_ref[half] = mlcol[...].T[j * 8 : j * 8 + 8]
 
+    add_late(0)
     second_send(0, 0, t_opp, e_opp)
     put(12, t_opp.at[0], w_opp0, up_v)
     put(13, e_opp.at[0], f_opp0, up_v)
     second_send(0, 1, t_opp, e_opp)
     put(14, t_opp.at[1], w_opp1, dn_v)
     put(15, e_opp.at[1], f_opp1, dn_v)
+    add_late(1)
     second_send(1, 1, t_up, e_up)
     put(16, t_up.at[1], w_up.at[1], up_v)
     put(17, e_up.at[1], f_up.at[1], up_v)
+    add_late(2)
     second_send(2, 0, t_dn, e_dn)
     put(20, t_dn.at[0], w_dn.at[0], dn_v)
     put(21, e_dn.at[0], f_dn.at[0], dn_v)
@@ -614,6 +623,7 @@
     second_send(2, 1, t_dn, e_dn, (w_opp1, f_opp1))
     put(22, t_dn.at[1], w_dn.at[1], dn_v)
     put(23, e_dn.at[1], f_dn.at[1], dn_v)
+    add_late(3)
 
     for half in (1, 0):
         get(16 if half else 18, w_up.at[half])
@@ -707,7 +717,7 @@
         + [pltpu.VMEM((2, 8, 128), F32)] * 3
         + [pltpu.VMEM((8, 128), F32)] * 2
         + [pltpu.VMEM((2, 8, 128), F32)] * 2
-        + [dma((32,)), dma((2, 20)), dma((24,)), dma((24,))],
+        + [dma((32,)), dma((2, 24)), dma((24,)), dma((24,))],
         compiler_params=pltpu.CompilerParams(
             collective_id=1, has_side_effects=True, vmem_limit_bytes=60 * 1024 * 1024
         ),

time: 164 us -> 152 us (0.927)
  Pallas kernels: 154 us -> 142 us
    pallas_call x1, Pallas kernels: 85 us -> 72.5 us  [body(): pl.pallas_call(attend_kernel, out_shape=jax.ShapeDtypeStruct((rows, heads...]
where the time goes in v3:
time: 152 us; the launch traced here: 151 us
  Pallas kernels  142 us (93%)
  local copies, waits for them, and re-layouts  8.17 us (5%)
    pallas_call x1, Pallas kernels, body(): pl.pallas_call(attend_kernel, out_shape=jax.ShapeDtypeStruct((rows, heads...  72.5 us
    pallas_call x1, Pallas kernels, body(): pl.pallas_call(gather_kernel, out_shape=(jax.ShapeDtypeStruct((16,) + qw....  69 us
    unnamed x11, local copies, waits for them, and re-layouts  5.92 us

profile of v3, /device:TPU:6, one launch (start us, length us, event | category | flops | bytes accessed | tf_op | source)
XLA Modules:
  0.0 151.3 jit_solution(13562857461419733361)
XLA Ops:
  0.6 0.0 copy-start.3
  0.6 0.0 copy-start
  0.6 0.9 copy.13
  1.5 0.9 fusion.1.iq_ref
  2.4 0.9 slice.7
  3.2 0.1 copy.12
  3.4 1.1 slice.6
  4.4 0.2 copy.14
  4.7 0.0 copy-done.3
  4.7 0.0 copy-done
  4.7 0.0 copy-start.1
  4.7 1.2 copy-done.1
  6.0 69.0 %gather.1 = (bf16[16,128,2304]{2,1,0:T(8,128)(2,1)}, bf16[8,576,1024]{2,1,0:T(8,128)(2,1)}, bf16[16,16,128]{2,1,0:T(8,128)(2,1)S(1)}, f32[128,4096]{1,0:T(8,128)S(1)}) custom-call(bf16[128,2304]{1,0:T(8,128)(2,1)S(1)} %pad_maximum_fusion.q_ref, bf16[576,1024]{1,0:T(8,128)(2,1)S(1)} %bitcast.9, bf16[320,128]{1,0:T(8,128)(2,1)S(1)} %fusion.1.iq_ref, ...), custom_call_target="tpu_custom_call" | custom-call | tf_op jit(solution)/shard_map/gather/pallas_call | solution.py:665
  75.0 0.0 copy-start.2
  75.0 0.6 copy-done.2
  75.6 72.5 %attend.1 = bf16[4,128,512]{2,1,0:T(8,128)(2,1)} custom-call(bf16[16,128,2304]{2,1,0:T(8,128)(2,1)} %get-tuple-element.6.qall, bf16[8,576,1024]{2,1,0:T(8,128)(2,1)} %get-tuple-element.7.kall, bf16[16,16,128]{2,1,0:T(8,128)(2,1)} %copy-done.2), custom_call_target="tpu_custom_call" | custom-call | tf_op jit(solution)/shard_map/attend/pallas_call | solution.py:692
  148.1 1.9 %copy.17 = bf16[4,128,512]{2,1,0:T(8,128)(2,1)} copy(bf16[4,128,512]{2,1,0:T(8,128)(2,1)} %attend.1) | data formatting | bytes 1048576
  150.0 1.3 copy.18
  (1 shorter events, 0.0 us)
Async XLA Ops:
  0.6 4.1 %copy-start.3 = (s32[4,2048]{1,0:T(4,128)S(1)}, s32[4,2048]{1,0:T(4,128)}, u32[]{:S(2)}) copy-start(s32[4,2048]{1,0:T(4,128)} %sel_ref.1) | copy-start | bytes 98308
  0.6 4.1 %copy-start = (bf16[1024,576]{0,1:T(8,128)(2,1)S(1)}, bf16[1024,576]{0,1:T(8,128)(2,1)}, u32[]{:S(2)}) copy-start(bf16[1024,576]{0,1:T(8,128)(2,1)} %param.6) | copy-start | bytes 3538948
  4.7 1.2 copy-start.1
  75.0 0.6 copy-start.2

commit v4 on v3

--- a/solution.py
+++ b/solution.py
@@ -103,11 +103,12 @@
             copy.wait_send()
 
 
-def gather_kernel(
+def kernel(
     q_ref, k_ref, iq_ref, keys_hbm, sel_ref,
-    qall, kall, tall, isc_ref,
-    iqall, tsend, gate_ref, keys_ref, logit_ref,
+    qall, isc_ref, out_ref,
+    kext, tall, iqall, tsend, gate_ref, keys_ref, logit_ref,
     q_send, q_recv, i_send, i_recv, p_send, p_recv, k_send, k_recv, t_send, t_recv, local,
+    *attend_refs,
 ):
     ctx, z = lax.axis_index("ctx"), lax.axis_index("row")
     core, chip = ctx % 2, ctx // 2
@@ -117,6 +118,13 @@
 
     keys_copy = pltpu.make_async_copy(keys_hbm, keys_ref, local.at[4])
     keys_copy.start()
+    ones = jnp.where(lax.broadcasted_iota(jnp.int32, (64, 1024), 0) == 0, 1.0, 0.0).astype(BF16)
+
+    def set_ones(block, carry):
+        kext[block, pl.ds(576, 64), :] = ones
+        return carry
+
+    lax.fori_loop(0, 8, set_ones, 0)
     barrier = pltpu.get_barrier_semaphore()
     for step in range(1, 16):
         pl.semaphore_signal(
@@ -148,7 +156,7 @@
     k_sent = []
 
     def k_view(depth, part, c=core):
-        return kall.at[c * 4 + depth % 4, parts[part]]
+        return kext.at[c * 4 + depth % 4, parts[part]]
 
     def k_put(k, src, dst, device):
         copy = remote(src, dst, k_send.at[k], k_recv.at[k], device)
@@ -318,8 +326,6 @@
     k_put(8, k_view(z + 2, 2), k_view(z + 2, 2), partner)
     index_chips(3, 7, *rest)
 
-    for j in range(4):
-        query_ring.last(j)
     k_get(4, z, 0, other)
     k_get(5, z + 3, 0, other)
     k_get(6, z + 1, 0, other)
@@ -332,20 +338,26 @@
         ).wait_recv()
     for copy in own[1:]:
         copy.wait()
+
+    def queries_here():
+        for j in range(4):
+            query_ring.last(j)
+
+    attend(qall, kext, tall, out_ref, queries_here, *attend_refs)
     query_ring.finish()
     index_ring.finish()
     for copy in to_partner + table_copies + k_sent:
         copy.wait_send()
 
 
-def attend_kernel(
-    qall, kall, tall, out_ref,
-    kext, ksel, qbuf, rope, raw, picks, mlcol, mlin,
+def attend(
+    qall, kext, tall, out_ref, queries_here,
+    ksel, qbuf, rope, raw, picks, mlcol, mlin,
     s_opp, s_up, s_dn, r_opp0, r_opp1, r_up, r_dn,
     m_opp, m_up, m_dn, n_opp0, n_opp1, n_up, n_dn,
     acc, t_opp, t_up, t_dn, w_opp0, w_opp1, w_up, w_dn,
     e_opp, e_up, e_dn, f_opp0, f_opp1, f_up, f_dn,
-    k_sem, q_sem, send, recv,
+    q_sem, send, recv,
 ):
     ctx = lax.axis_index("ctx")
     core = ctx % 2
@@ -355,14 +367,6 @@
     up_v = {"ctx": chip_of(u, v + 1, core) * 2 + core}
     dn_v = {"ctx": chip_of(u, v + 3, core) * 2 + core}
     order = (2, 1, 3, 0)
-
-    barrier = pltpu.get_barrier_semaphore()
-    for device in (up_u, dn_u, up_v, dn_v):
-        pl.semaphore_signal(barrier, inc=1, device_id=device, device_id_type=MESH)
-
-    def k_copy(w):
-        at = pl.ds(pl.multiple_of((w % 4) * 256, 256), 256)
-        return pltpu.make_async_copy(kall.at[w // 4, :, at], kext.at[w, pl.ds(0, 576), :], k_sem.at[w])
 
     groups = ((2, 2), (3, 1), (1, 3), (0, 0))
 
@@ -384,21 +388,6 @@
             pltpu.make_async_copy(src, dst, q_sem.at[group % 2, n]) for n, (src, dst) in enumerate(copies)
         ]
 
-    def start_k(w, carry):
-        k_copy(w).start()
-        return carry
-
-    lax.fori_loop(0, 32, start_k, 0)
-    for copy in q_copies(0):
-        copy.start()
-
-    ones = jnp.where(lax.broadcasted_iota(jnp.int32, (64, 256), 0) == 0, 1.0, 0.0).astype(BF16)
-
-    def set_ones(w, carry):
-        kext[w, pl.ds(576, 64), :] = ones
-        return carry
-
-    lax.fori_loop(0, 32, set_ones, 0)
     probe = jnp.where(lax.broadcasted_iota(jnp.int32, (16, 640), 1) == 576, 1.0, 0.0).astype(BF16)
 
     def set_probe(row, carry):
@@ -407,8 +396,6 @@
         return carry
 
     lax.fori_loop(0, 16, set_probe, 0)
-    pl.semaphore_wait(barrier, 4)
-
     sent = []
 
     def put(k, src, dst, device):
@@ -451,13 +438,11 @@
         def some_windows(i, carry):
             for step in range(4):
                 w = i * 4 + step
-                if chunk == 0:
-                    k_copy(w).wait()
-            for step in range(4):
-                w = i * 4 + step
                 want = jnp.sum(jnp.where(wide == w, picks[...], 0.0), axis=1, keepdims=True)
                 onehot = jnp.where(token == want, 1.0, 0.0).astype(BF16)
-                rows = lax.dot_general(onehot, kext[w], NT, preferred_element_type=F32)
+                rows = lax.dot_general(
+                    onehot, kext[i, :, step * 256 : (step + 1) * 256], NT, preferred_element_type=F32
+                )
                 at = pl.ds(pl.multiple_of(w * 16, 16), 16)
                 ksel[:, at, :] = rows.astype(BF16).reshape(16, 16, 640)
             return carry
@@ -516,13 +501,19 @@
     mlcol[...] = jnp.zeros((128, 128), F32)
 
     def next_chunk(chunk):
+        if chunk == 0:
+            gather_tokens(chunk)
+            queries_here()
+            for copy in q_copies(chunk):
+                copy.start()
         for copy in q_copies(chunk):
             copy.wait()
         if chunk < 3:
             for copy in q_copies(chunk + 1):
                 copy.start()
         set_rope(chunk % 2)
-        gather_tokens(chunk)
+        if chunk:
+            gather_tokens(chunk)
 
     next_chunk(0)
     send_half(0, 0, s_opp, m_opp, ())
@@ -662,17 +653,20 @@
     iqg = jnp.concatenate([index_query.reshape(-1, 128), gates], axis=0)
     dma = pltpu.SemaphoreType.DMA
 
-    qall, kall, tall, index_scores = pl.pallas_call(
-        gather_kernel,
+    half = (4, 2, heads, LATENT)
+    quarter = (2, heads, LATENT)
+    _, index_scores, attended = pl.pallas_call(
+        kernel,
         out_shape=(
             jax.ShapeDtypeStruct((16,) + qw.shape, BF16),
-            jax.ShapeDtypeStruct((8, width, tokens), BF16),
-            jax.ShapeDtypeStruct((16, 16, 128), BF16),
             jax.ShapeDtypeStruct((rows * 32, index_keys.shape[0]), F32),
+            jax.ShapeDtypeStruct((rows, heads, LATENT), BF16),
         ),
         in_specs=[vmem(), vmem(), vmem(), anywhere(), vmem()],
-        out_specs=(anywhere(), anywhere(), anywhere(), vmem()),
+        out_specs=(anywhere(), vmem(), vmem()),
         scratch_shapes=[
+            pltpu.VMEM((8, 640, tokens), BF16),
+            pltpu.VMEM((16, 16, 128), BF16),
             pltpu.VMEM((16, 2) + iqg.shape, BF16),
             pltpu.VMEM((16, 16, 128), BF16),
             pltpu.VMEM((512, 128), F32),
@@ -680,22 +674,6 @@
             pltpu.VMEM((2, 512, 512), F32),
             dma((20,)), dma((20,)), dma((20,)), dma((20,)), dma((21,)), dma((21,)),
             dma((9,)), dma((9,)), dma((16,)), dma((16,)), dma((5,)),
-        ],
-        compiler_params=pltpu.CompilerParams(
-            collective_id=0, has_side_effects=True, vmem_limit_bytes=48 * 1024 * 1024
-        ),
-        name="gather",
-    )(qw, kt, iqg, index_keys, selected)
-
-    half = (4, 2, heads, LATENT)
-    quarter = (2, heads, LATENT)
-    attended = pl.pallas_call(
-        attend_kernel,
-        out_shape=jax.ShapeDtypeStruct((rows, heads, LATENT), BF16),
-        in_specs=[anywhere(), anywhere(), vmem()],
-        out_specs=vmem(),
-        scratch_shapes=[
-            pltpu.VMEM((32, 640, 256), BF16),
             pltpu.VMEM((16, 512, 640), BF16),
             pltpu.VMEM((2, 16, 144, 640), BF16),
             pltpu.VMEM((2, 4, heads, 256), BF16),
@@ -717,12 +695,12 @@
         + [pltpu.VMEM((2, 8, 128), F32)] * 3
         + [pltpu.VMEM((8, 128), F32)] * 2
         + [pltpu.VMEM((2, 8, 128), F32)] * 2
-        + [dma((32,)), dma((2, 24)), dma((24,)), dma((24,))],
+        + [dma((2, 24)), dma((24,)), dma((24,))],
         compiler_params=pltpu.CompilerParams(
-            collective_id=1, has_side_effects=True, vmem_limit_bytes=60 * 1024 * 1024
+            collective_id=0, has_side_effects=True, vmem_limit_bytes=63 * 1024 * 1024
         ),
         name="attend",
-    )(qall, kall, tall)
+    )(qw, kt, iqg, index_keys, selected)
     return attended, index_scores
 
 

time: 152 us -> 150 us (0.987)
  Pallas kernels: 142 us -> 139 us
    pallas_call x2 -> x1, Pallas kernels: 142 us -> 139 us  [body(): pl.pallas_call(kernel, out_shape=(jax.ShapeDtypeStruct((16,) + qw.shape,...]
    unnamed x11 -> x3, local copies, waits for them, and re-layouts: 5.92 us -> 5.82 us
where the time goes in v4:
time: 150 us; the launch traced here: 149 us
  Pallas kernels  139 us (93%)
  local copies, waits for them, and re-layouts  6.99 us (5%)
  other arithmetic  2.34 us (2%)
    pallas_call x1, Pallas kernels, body(): pl.pallas_call(kernel, out_shape=(jax.ShapeDtypeStruct((16,) + qw.shape,...  139 us
    unnamed x3, local copies, waits for them, and re-layouts  5.82 us

profile of v4, /device:TPU:6, one launch (start us, length us, event | category | flops | bytes accessed | tf_op | source)
XLA Modules:
  0.0 149.2 jit_solution(8321166140061966900)
XLA Ops:
  0.6 0.0 slice-start
  0.6 0.8 copy.13
  1.5 1.5 fusion.1.iq_ref
  3.0 0.8 slice.7
  3.8 0.1 copy.12
  3.9 0.0 slice-done
  3.9 0.2 copy.14
  4.2 0.9 pad_maximum_fusion.q_ref
  5.0 139.2 %attend.1 = (bf16[16,128,2304]{2,1,0:T(8,128)(2,1)}, f32[128,4096]{1,0:T(8,128)}, bf16[4,128,512]{2,1,0:T(8,128)(2,1)}) custom-call(bf16[128,2304]{1,0:T(8,128)(2,1)} %pad_maximum_fusion.q_ref, bf16[576,1024]{1,0:T(8,128)(2,1)} %bitcast.10, bf16[320,128]{1,0:T(8,128)(2,1)} %fusion.1.iq_ref, bf16[4096,128]{1,0:T(8,128)(2,1)} %keys_hbm.1, s32[4,2048]{1,0:T(4,128)} %sel_ref.1), custom_call_target="tpu_custom_call" | custom-call | tf_op jit(solution)/shard_map/attend/pallas_call | solution.py:658
  144.2 1.9 %copy.17 = bf16[4,128,512]{2,1,0:T(8,128)(2,1)} copy(bf16[4,128,512]{2,1,0:T(8,128)(2,1)} %get-tuple-element.8) | data formatting | bytes 1048576
  146.1 3.1 %copy.18 = f32[128,4096]{1,0:T(8,128)} copy(f32[128,4096]{1,0:T(8,128)} %get-tuple-element.9) | data formatting | bytes 4194304
Async XLA Ops:
  0.6 3.3 %slice-start = ((bf16[4,128,576]{1,2,0:T(8,128)(2,1)}), bf16[4,128,512]{1,2,0:T(8,128)(2,1)S(1)}, s32[]{:S(2)}) async-start(bf16[4,128,576]{1,2,0:T(8,128)(2,1)} %param.8), calls=%async_computation | async-start | bytes 1048576 | tf_op jit(solution)/shard_map/slice | solution.py:649

commit v5 on v4

--- a/solution.py
+++ b/solution.py
@@ -287,11 +287,11 @@
     index_ring.near()
     send_tables()
     index_ring.relay(0)
-    index_ring.far()
     own[0].wait()
     keys_copy.wait()
     wait_partner(0, 0)
     index_chips(0, 1, lambda k: k, lambda k: k)
+    index_ring.far()
     index_ring.relay(1)
     index_ring.relay(2)
     index_ring.last(0)

time: 150 us -> 150 us (level)
  no operation moved by 1% of the time
where the time goes in v5:
time: 150 us; the launch traced here: 149 us
  Pallas kernels  139 us (93%)
  local copies, waits for them, and re-layouts  6.99 us (5%)
  other arithmetic  2.34 us (2%)
    pallas_call x1, Pallas kernels, body(): pl.pallas_call(kernel, out_shape=(jax.ShapeDtypeStruct((16,) + qw.shape,...  139 us
    unnamed x3, local copies, waits for them, and re-layouts  5.82 us

profile of v5, /device:TPU:6, one launch (start us, length us, event | category | flops | bytes accessed | tf_op | source)
XLA Modules:
  0.0 149.2 jit_solution(5099721749333687236)
XLA Ops:
  0.6 0.0 slice-start
  0.6 0.8 copy.13
  1.5 1.5 fusion.1.iq_ref
  3.0 0.8 slice.7
  3.8 0.1 copy.12
  3.9 0.0 slice-done
  3.9 0.2 copy.14
  4.2 0.9 pad_maximum_fusion.q_ref
  5.0 139.2 %attend.1 = (bf16[16,128,2304]{2,1,0:T(8,128)(2,1)}, f32[128,4096]{1,0:T(8,128)}, bf16[4,128,512]{2,1,0:T(8,128)(2,1)}) custom-call(bf16[128,2304]{1,0:T(8,128)(2,1)} %pad_maximum_fusion.q_ref, bf16[576,1024]{1,0:T(8,128)(2,1)} %bitcast.10, bf16[320,128]{1,0:T(8,128)(2,1)} %fusion.1.iq_ref, bf16[4096,128]{1,0:T(8,128)(2,1)} %keys_hbm.1, s32[4,2048]{1,0:T(4,128)} %sel_ref.1), custom_call_target="tpu_custom_call" | custom-call | tf_op jit(solution)/shard_map/attend/pallas_call | solution.py:658
  144.2 1.9 %copy.17 = bf16[4,128,512]{2,1,0:T(8,128)(2,1)} copy(bf16[4,128,512]{2,1,0:T(8,128)(2,1)} %get-tuple-element.8) | data formatting | bytes 1048576
  146.1 3.1 %copy.18 = f32[128,4096]{1,0:T(8,128)} copy(f32[128,4096]{1,0:T(8,128)} %get-tuple-element.9) | data formatting | bytes 4194304
Async XLA Ops:
  0.6 3.3 %slice-start = ((bf16[4,128,576]{1,2,0:T(8,128)(2,1)}), bf16[4,128,512]{1,2,0:T(8,128)(2,1)S(1)}, s32[]{:S(2)}) async-start(bf16[4,128,576]{1,2,0:T(8,128)(2,1)} %param.8), calls=%async_computation | async-start | bytes 1048576 | tf_op jit(solution)/shard_map/slice | solution.py:649
